TPU v7x, 256 devices: a whole 4x4x8 slice. The times are simulated.
256 devices in a mesh: blk: 32 (over y, x, z_hi), rows: 8 (over z_lo, core).
Axes of the slice: x: 4, y: 4, z: 8 (z_hi: 2, z_lo: 4; z = z_hi * 4 + z_lo), core: 2. Of those that a mesh axis runs over, the one named last changes fastest.
Arguments:
- target_pos: float32 [3, 65536], P(None, ('blk', 'rows')), may hold values from 0 to 5.03852
- target_len: float32 [65536], P(('blk', 'rows')), may hold values from 0.2 to 0.6
- cotangent: float32 [65536, 128], P(('blk', 'rows')), may hold values from -0.3125 to 0.3125
- source_pos: float32 [3, 32768], P(None, ('blk', 'rows')), may hold values from 0 to 5.03852
- source_len: float32 [32768], P(('blk', 'rows')), may hold values from 0.2 to 0.6
- vectors: float32 [32768, 128], P(('blk', 'rows')), may hold values from -6 to 6
Outputs:
- grad_vectors: float32 [32768, 128], P(('blk', 'rows'))
- grad_source_len: float32 [32768], P(('blk', 'rows'))
- grad_target_len: float32 [65536], P(('blk', 'rows'))
All inputs are finite; a program needn't handle non-finite values.
Results may differ from a plain program's by a relative error of at most 0.0003.
Values sent between devices are 32-bit elements; how exact they have to be, the bound alone decides.
No kernel may reach another device: no remote copies, remote signals or barrier semaphores. Data moves between devices by JAX's collectives and lax.ppermute only.
A program may use at most 64 MiB of HBM per device.

v0:
```python
import jax
import jax.numpy as jnp
from jax import lax
from jax.sharding import PartitionSpec as P

STEPS = 8


def passed_along(block, axis, distance):
    devices = range(lax.axis_size(axis))
    route = [((i - distance) % len(devices), i) for i in devices]
    return lax.ppermute(block, axis, route)


def pair_terms(target_pos, target_len, cotangent, source_pos, source_len, vectors):
    dist_sq = jnp.zeros((target_len.shape[0], source_len.shape[0]), jnp.float32)
    for component in range(3):
        offset = target_pos[component][:, None] - source_pos[component][None, :]
        dist_sq = dist_sq + offset * offset
    scale_sum = (
        target_len[:, None] * target_len[:, None] + source_len[None, :] * source_len[None, :]
    )
    length_ratio = 2.0 * target_len[:, None] * source_len[None, :] / scale_sum
    kernel = length_ratio * jnp.sqrt(length_ratio) * jnp.exp(-dist_sq / scale_sum)
    products = jnp.dot(cotangent, vectors.T, precision=lax.Precision.HIGHEST)
    weighted = products * kernel
    shaped = weighted / scale_sum * (2.0 * dist_sq / scale_sum - 3.0)
    grad_target = target_len * jnp.sum(shaped, 1) + 1.5 / target_len * jnp.sum(weighted, 1)
    grad_source = source_len * jnp.sum(shaped, 0) + 1.5 / source_len * jnp.sum(weighted, 0)
    grad_vec = jnp.dot(kernel.T, cotangent, precision=lax.Precision.HIGHEST)
    return (grad_target, grad_vec, grad_source)


def tile_terms(target_pos, target_len, cotangent, source_block):
    source_pos, source_len, vectors = source_block
    block_size = source_len.shape[0]
    tile_width = min(512, block_size)
    tile_count = block_size // tile_width
    pos_tiles = jnp.transpose(source_pos.reshape(3, tile_count, tile_width), (1, 0, 2))
    len_tiles = source_len.reshape(tile_count, tile_width)
    vec_tiles = vectors.reshape(tile_count, tile_width, vectors.shape[1])

    def per_tile(pieces):
        return pair_terms(target_pos, target_len, cotangent, pieces[0], pieces[1], pieces[2])

    target_parts, vec_parts, source_parts = lax.map(per_tile, (pos_tiles, len_tiles, vec_tiles))
    return (
        jnp.sum(target_parts, 0),
        vec_parts.reshape(block_size, vectors.shape[1]),
        source_parts.reshape(block_size),
    )


def shards(target_pos, target_len, cotangent, source_pos, source_len, vectors):
    grad_target_len = jnp.zeros(target_len.shape, jnp.float32)
    source_block = (
        lax.all_gather(source_pos, "rows", axis=1, tiled=True),
        lax.all_gather(source_len, "rows", axis=0, tiled=True),
        lax.all_gather(vectors, "rows", axis=0, tiled=True),
    )
    sum_vec = jnp.zeros(source_block[2].shape, jnp.float32)
    sum_len = jnp.zeros(source_block[1].shape, jnp.float32)
    for cycle_step in range(STEPS):
        current = source_block
        if cycle_step + 1 < STEPS:
            source_block = passed_along(
                (source_block[0], source_block[1], source_block[2]), "blk", 1
            )
        grad_target, grad_vec, grad_source = tile_terms(target_pos, target_len, cotangent, current)
        grad_target_len = grad_target_len + grad_target
        sum_vec = sum_vec + grad_vec
        sum_len = sum_len + grad_source
        if cycle_step + 1 < STEPS:
            sum_vec, sum_len = passed_along((sum_vec, sum_len), "blk", 1)
    share_vec, share_len = (
        lax.psum_scatter(sum_vec, "rows", scatter_dimension=0, tiled=True),
        lax.psum_scatter(sum_len, "rows", scatter_dimension=0, tiled=True),
    )
    grad_vectors, grad_source_len = passed_along((share_vec, share_len), "blk", -(STEPS - 1))
    return (grad_vectors, grad_source_len, grad_target_len)


def solution(mesh):
    placed = (
        P(None, ("blk", "rows")),
        P(("blk", "rows")),
        P(("blk", "rows"), None),
        P(None, ("blk", "rows")),
        P(("blk", "rows")),
        P(("blk", "rows"), None),
    )
    return jax.shard_map(
        shards,
        mesh=mesh,
        in_specs=placed,
        out_specs=(P(("blk", "rows"), None), P(("blk", "rows")), P(("blk", "rows"))),
        check_vma=False,
    )
```

profile of v0, /device:TPU:1, one launch (start us, length us, event | category | flops | bytes accessed | tf_op | source)
XLA Modules:
  0.0 580.9 jit_solution(9542216574656629737)
XLA Ops:
  7.2 15.9 %all_gather.11 = f32[3,1024]{1,0:T(4,128)S(1)} all-gather(f32[3,128]{1,0:T(4,128)} %param.25), channel_id=1, replica_groups=mesh['blk'=32,'rows'=8] {'rows'}, dimensions={1}, use_global_device_ids=true | all-gather | bytes 13824 | tf_op jit(solution)/shard_map/all_gather | solution.py:57
  44.9 12.0 %all-gather = f32[8,1,128]{2,1,0:T(1,128)S(1)} all-gather(f32[1,1,128]{2,1,0:T(1,128)S(1)} %bitcast.733), channel_id=1, replica_groups=mesh['blk'=32,'rows'=8] {'rows'}, dimensions={0}, use_global_device_ids=true | all-gather | bytes 4608 | tf_op jit(solution)/shard_map/all_gather | solution.py:58
  56.9 10.9 %collective-permute-done.2 = f32[1024]{0:T(1024)S(1)} collective-permute-done((f32[1024]{0:T(1024)S(1)}, f32[1024]{0:T(1024)S(1)}, u32[]{:S(2)}, u32[]{:S(2)}) %collective-permute-start.2) | collective-permute-done | bytes 4128 | tf_op jit(solution)/shard_map/ppermute | solution.py:12
  67.8 10.6 %collective-permute-done.6 = f32[1024]{0:T(1024)S(1)} collective-permute-done((f32[1024]{0:T(1024)S(1)}, f32[1024]{0:T(1024)S(1)}, u32[]{:S(2)}, u32[]{:S(2)}) %collective-permute-start.6) | collective-permute-done | bytes 4128 | tf_op jit(solution)/shard_map/ppermute | solution.py:12
  78.4 10.7 %collective-permute-done.10 = f32[1024]{0:T(1024)S(1)} collective-permute-done((f32[1024]{0:T(1024)S(1)}, f32[1024]{0:T(1024)S(1)}, u32[]{:S(2)}, u32[]{:S(2)}) %collective-permute-start.10) | collective-permute-done | bytes 4128 | tf_op jit(solution)/shard_map/ppermute | solution.py:12
  89.0 10.6 %collective-permute-done.14 = f32[1024]{0:T(1024)S(1)} collective-permute-done((f32[1024]{0:T(1024)S(1)}, f32[1024]{0:T(1024)S(1)}, u32[]{:S(2)}, u32[]{:S(2)}) %collective-permute-start.14) | collective-permute-done | bytes 4128 | tf_op jit(solution)/shard_map/ppermute | solution.py:12
  99.6 10.6 %collective-permute-done.18 = f32[1024]{0:T(1024)S(1)} collective-permute-done((f32[1024]{0:T(1024)S(1)}, f32[1024]{0:T(1024)S(1)}, u32[]{:S(2)}, u32[]{:S(2)}) %collective-permute-start.18) | collective-permute-done | bytes 4128 | tf_op jit(solution)/shard_map/ppermute | solution.py:12
  110.2 21.3 %all_gather.9 = f32[1024,128]{1,0:T(8,128)} all-gather(f32[128,128]{1,0:T(8,128)} %param.27), channel_id=1, replica_groups=mesh['blk'=32,'rows'=8] {'rows'}, dimensions={0}, use_global_device_ids=true | all-gather | bytes 589824 | tf_op jit(solution)/shard_map/all_gather | solution.py:59
  144.0 26.2 %collective-permute-done.26 = f32[1024]{0:T(1024)S(1)} collective-permute-done((f32[1024]{0:T(1024)S(1)}, f32[1024]{0:T(1024)S(1)}, u32[]{:S(2)}, u32[]{:S(2)}) %collective-permute-start.26) | collective-permute-done | bytes 4128 | tf_op jit(solution)/shard_map/ppermute | solution.py:12
  188.2 37.9 %collective-permute-done.5 = f32[1024,128]{1,0:T(8,128)} collective-permute-done((f32[1024,128]{1,0:T(8,128)}, f32[1024,128]{1,0:T(8,128)}, u32[]{:S(2)}, u32[]{:S(2)}) %collective-permute-start.5) | collective-permute-done | bytes 524320 | tf_op jit(solution)/shard_map/ppermute | solution.py:12
  237.4 19.6 %collective-permute-done.9 = f32[1024,128]{1,0:T(8,128)} collective-permute-done((f32[1024,128]{1,0:T(8,128)}, f32[1024,128]{1,0:T(8,128)}, u32[]{:S(2)}, u32[]{:S(2)}) %collective-permute-start.9) | collective-permute-done | bytes 524320 | tf_op jit(solution)/shard_map/ppermute | solution.py:12
  274.5 35.4 %collective-permute-done.13 = f32[1024,128]{1,0:T(8,128)} collective-permute-done((f32[1024,128]{1,0:T(8,128)}, f32[1024,128]{1,0:T(8,128)}, u32[]{:S(2)}, u32[]{:S(2)}) %collective-permute-start.13) | collective-permute-done | bytes 524320 | tf_op jit(solution)/shard_map/ppermute | solution.py:12
  316.4 17.6 %collective-permute-done.12 = f32[1024,128]{1,0:T(8,128)S(1)} collective-permute-done((f32[1024,128]{1,0:T(8,128)S(1)}, f32[1024,128]{1,0:T(8,128)S(1)}, u32[]{:S(2)}, u32[]{:S(2)}) %collective-permute-start.12) | collective-permute-done | bytes 524320 | tf_op jit(solution)/shard_map/ppermute | solution.py:12
  340.2 34.2 %collective-permute-done.17 = f32[1024,128]{1,0:T(8,128)} collective-permute-done((f32[1024,128]{1,0:T(8,128)}, f32[1024,128]{1,0:T(8,128)}, u32[]{:S(2)}, u32[]{:S(2)}) %collective-permute-start.17) | collective-permute-done | bytes 524320 | tf_op jit(solution)/shard_map/ppermute | solution.py:12
  380.9 14.3 %collective-permute-done.16 = f32[1024,128]{1,0:T(8,128)S(1)} collective-permute-done((f32[1024,128]{1,0:T(8,128)S(1)}, f32[1024,128]{1,0:T(8,128)S(1)}, u32[]{:S(2)}, u32[]{:S(2)}) %collective-permute-start.16) | collective-permute-done | bytes 524320 | tf_op jit(solution)/shard_map/ppermute | solution.py:12
  395.3 21.1 %collective-permute-done.21 = f32[1024,128]{1,0:T(8,128)} collective-permute-done((f32[1024,128]{1,0:T(8,128)}, f32[1024,128]{1,0:T(8,128)}, u32[]{:S(2)}, u32[]{:S(2)}) %collective-permute-start.21) | collective-permute-done | bytes 524320 | tf_op jit(solution)/shard_map/ppermute | solution.py:12
  424.7 17.5 %collective-permute-done.20 = f32[1024,128]{1,0:T(8,128)S(1)} collective-permute-done((f32[1024,128]{1,0:T(8,128)S(1)}, f32[1024,128]{1,0:T(8,128)S(1)}, u32[]{:S(2)}, u32[]{:S(2)}) %collective-permute-start.20) | collective-permute-done | bytes 524320 | tf_op jit(solution)/shard_map/ppermute | solution.py:12
  442.4 11.4 %collective-permute-done.25 = f32[1024,128]{1,0:T(8,128)S(1)} collective-permute-done((f32[1024,128]{1,0:T(8,128)}, f32[1024,128]{1,0:T(8,128)S(1)}, u32[]{:S(2)}, u32[]{:S(2)}) %collective-permute-start.25) | collective-permute-done | bytes 524320 | tf_op jit(solution)/shard_map/ppermute | solution.py:12
  476.5 10.6 %collective-permute-done.30 = f32[1024]{0:T(1024)S(1)} collective-permute-done((f32[1024]{0:T(1024)S(1)}, f32[1024]{0:T(1024)S(1)}, u32[]{:S(2)}, u32[]{:S(2)}) %collective-permute-start.30) | collective-permute-done | bytes 4128 | tf_op jit(solution)/shard_map/ppermute | solution.py:12
  487.1 10.7 %collective-permute-done.31 = f32[1024]{0:T(1024)S(1)} collective-permute-done((f32[1024]{0:T(1024)S(1)}, f32[1024]{0:T(1024)S(1)}, u32[]{:S(2)}, u32[]{:S(2)}) %collective-permute-start.31) | collective-permute-done | bytes 4128 | tf_op jit(solution)/shard_map/ppermute | solution.py:12
  497.8 10.6 %collective-permute-done.32 = f32[1024]{0:T(1024)S(1)} collective-permute-done((f32[1024]{0:T(1024)S(1)}, f32[1024]{0:T(1024)S(1)}, u32[]{:S(2)}, u32[]{:S(2)}) %collective-permute-start.32) | collective-permute-done | bytes 4128 | tf_op jit(solution)/shard_map/ppermute | solution.py:12
  508.4 10.6 %collective-permute-done.33 = f32[1024]{0:T(1024)S(1)} collective-permute-done((f32[1024]{0:T(1024)S(1)}, f32[1024]{0:T(1024)S(1)}, u32[]{:S(2)}, u32[]{:S(2)}) %collective-permute-start.33) | collective-permute-done | bytes 4128 | tf_op jit(solution)/shard_map/ppermute | solution.py:12
  519.0 10.6 %collective-permute-done.34 = f32[1024]{0:T(1024)S(1)} collective-permute-done((f32[1024]{0:T(1024)S(1)}, f32[1024]{0:T(1024)S(1)}, u32[]{:S(2)}, u32[]{:S(2)}) %collective-permute-start.34) | collective-permute-done | bytes 4128 | tf_op jit(solution)/shard_map/ppermute | solution.py:12
  540.2 22.9 %all-reduce = f32[1024]{0:T(1024)S(1)} all-reduce(f32[1024]{0:T(1024)S(1)} %add.696), channel_id=3, replica_groups=mesh['blk'=32,'rows'=8] {'rows'}, use_global_device_ids=true, to_apply=%region_49.50.clone | all-reduce | flops 1024 | bytes 8192
  (329 shorter events, 201.7 us)
Async XLA Ops:
  7.2 556.1 %reduce-scatter.2.cloned.1.call-start = ((), (), s32[]{:S(2)}) async-start(), calls=%async_computation.1 | async-start | bytes 589824 | tf_op jit(solution)/shard_map/reduce_scatter | solution.py:76
  23.2 11.0 %collective-permute-start.3 = (f32[3,1024]{1,0:T(4,128)S(1)}, f32[3,1024]{1,0:T(4,128)S(1)}, u32[]{:S(2)}, u32[]{:S(2)}) collective-permute-start(f32[3,1024]{1,0:T(4,128)S(1)} %all_gather.11), channel_id=1, source_target_pairs={{248,0},{0,8},{8,16},{16,24},{24,32},{32,40},{40,48},{48,56},{56,6... | collective-permute-start | bytes 36872 | tf_op jit(solution)/shard_map/ppermute | solution.py:12
  44.9 33.5 %collective-permute-start.11 = (f32[3,1024]{1,0:T(4,128)S(1)}, f32[3,1024]{1,0:T(4,128)S(1)}, u32[]{:S(2)}, u32[]{:S(2)}) collective-permute-start(f32[3,1024]{1,0:T(4,128)S(1)} %collective-permute-done.7), channel_id=1, source_target_pairs={{248,0},{0,8},{8,16},{16,24},{24,32},{32,40},{40,48},{48,56},{56,6... | collective-permute-start | bytes 36872 | tf_op jit(solution)/shard_map/ppermute | solution.py:12
  56.9 10.9 %collective-permute-start.2 = (f32[1024]{0:T(1024)S(1)}, f32[1024]{0:T(1024)S(1)}, u32[]{:S(2)}, u32[]{:S(2)}) collective-permute-start(f32[1024]{0:T(1024)S(1)} %bitcast.706), channel_id=1, source_target_pairs={{248,0},{0,8},{8,16},{16,24},{24,32},{32,40},{40,48},{48,56},{56,6... | collective-permute-start | bytes 12296 | tf_op jit(solution)/shard_map/ppermute | solution.py:12
  78.4 31.9 %collective-permute-start.15 = (f32[3,1024]{1,0:T(4,128)S(1)}, f32[3,1024]{1,0:T(4,128)S(1)}, u32[]{:S(2)}, u32[]{:S(2)}) collective-permute-start(f32[3,1024]{1,0:T(4,128)S(1)} %collective-permute-done.11), channel_id=1, source_target_pairs={{248,0},{0,8},{8,16},{16,24},{24,32},{32,40},{40,48},{48,56},{56,6... | collective-permute-start | bytes 36872 | tf_op jit(solution)/shard_map/ppermute | solution.py:12
  110.2 23.2 %collective-permute-start.22 = (f32[1024]{0:T(1024)S(1)}, f32[1024]{0:T(1024)S(1)}, u32[]{:S(2)}, u32[]{:S(2)}) collective-permute-start(f32[1024]{0:T(1024)S(1)} %collective-permute-done.18), channel_id=1, source_target_pairs={{248,0},{0,8},{8,16},{16,24},{24,32},{32,40},{40,48},{48,56},{56,6... | collective-permute-start | bytes 12296 | tf_op jit(solution)/shard_map/ppermute | solution.py:12
  110.2 23.2 %collective-permute-start.19 = (f32[3,1024]{1,0:T(4,128)S(1)}, f32[3,1024]{1,0:T(4,128)S(1)}, u32[]{:S(2)}, u32[]{:S(2)}) collective-permute-start(f32[3,1024]{1,0:T(4,128)S(1)} %collective-permute-done.15), channel_id=1, source_target_pairs={{248,0},{0,8},{8,16},{16,24},{24,32},{32,40},{40,48},{48,56},{56,6... | collective-permute-start | bytes 36872 | tf_op jit(solution)/shard_map/ppermute | solution.py:12
  131.5 45.3 %collective-permute-start.1 = (f32[1024,128]{1,0:T(8,128)}, f32[1024,128]{1,0:T(8,128)}, u32[]{:S(2)}, u32[]{:S(2)}) collective-permute-start(f32[1024,128]{1,0:T(8,128)} %all_gather.9), channel_id=1, source_target_pairs={{248,0},{0,8},{8,16},{16,24},{24,32},{32,40},{40,48},{48,56},{56,6... | collective-permute-start | bytes 1572872 | tf_op jit(solution)/shard_map/ppermute | solution.py:12
  133.4 36.9 %collective-permute-start.26 = (f32[1024]{0:T(1024)S(1)}, f32[1024]{0:T(1024)S(1)}, u32[]{:S(2)}, u32[]{:S(2)}) collective-permute-start(f32[1024]{0:T(1024)S(1)} %collective-permute-done.22), channel_id=1, source_target_pairs={{248,0},{0,8},{8,16},{16,24},{24,32},{32,40},{40,48},{48,56},{56,6... | collective-permute-start | bytes 12296 | tf_op jit(solution)/shard_map/ppermute | solution.py:12
  133.4 37.2 %collective-permute-start.23 = (f32[3,1024]{1,0:T(4,128)S(1)}, f32[3,1024]{1,0:T(4,128)}, u32[]{:S(2)}, u32[]{:S(2)}) collective-permute-start(f32[3,1024]{1,0:T(4,128)S(1)} %collective-permute-done.19), channel_id=1, source_target_pairs={{248,0},{0,8},{8,16},{16,24},{24,32},{32,40},{40,48},{48,56},{56,6... | collective-permute-start | bytes 36872 | tf_op jit(solution)/shard_map/ppermute | solution.py:12
  141.1 42.3 %collective-permute-start = (f32[1024,128]{1,0:T(8,128)S(1)}, f32[1024,128]{1,0:T(8,128)S(1)}, u32[]{:S(2)}, u32[]{:S(2)}) collective-permute-start(f32[1024,128]{1,0:T(8,128)S(1)} %bitcast.539), channel_id=1, source_target_pairs={{248,0},{0,8},{8,16},{16,24},{24,32},{32,40},{40,48},{48,56},{56,6... | collective-permute-start | bytes 1572872 | tf_op jit(solution)/shard_map/ppermute | solution.py:12
  170.6 271.8 %collective-permute-start.27 = (f32[3,1024]{1,0:T(4,128)}, f32[3,1024]{1,0:T(4,128)S(1)}, u32[]{:S(2)}, u32[]{:S(2)}) collective-permute-start(f32[3,1024]{1,0:T(4,128)} %collective-permute-done.23), channel_id=1, source_target_pairs={{248,0},{0,8},{8,16},{16,24},{24,32},{32,40},{40,48},{48,56},{56,6... | collective-permute-start | bytes 36872 | tf_op jit(solution)/shard_map/ppermute | solution.py:12
  176.8 49.3 %collective-permute-start.5 = (f32[1024,128]{1,0:T(8,128)}, f32[1024,128]{1,0:T(8,128)}, u32[]{:S(2)}, u32[]{:S(2)}) collective-permute-start(f32[1024,128]{1,0:T(8,128)} %collective-permute-done.1), channel_id=1, source_target_pairs={{248,0},{0,8},{8,16},{16,24},{24,32},{32,40},{40,48},{48,56},{56,6... | collective-permute-start | bytes 1572872 | tf_op jit(solution)/shard_map/ppermute | solution.py:12
  183.4 53.9 %collective-permute-start.4 = (f32[1024,128]{1,0:T(8,128)S(1)}, f32[1024,128]{1,0:T(8,128)S(1)}, u32[]{:S(2)}, u32[]{:S(2)}) collective-permute-start(f32[1024,128]{1,0:T(8,128)S(1)} %bitcast_add_fusion.6), channel_id=1, source_target_pairs={{248,0},{0,8},{8,16},{16,24},{24,32},{32,40},{40,48},{48,56},{56,6... | collective-permute-start | bytes 1572872 | tf_op jit(solution)/shard_map/ppermute | solution.py:12
  226.1 30.9 %collective-permute-start.9 = (f32[1024,128]{1,0:T(8,128)}, f32[1024,128]{1,0:T(8,128)}, u32[]{:S(2)}, u32[]{:S(2)}) collective-permute-start(f32[1024,128]{1,0:T(8,128)} %collective-permute-done.5), channel_id=1, source_target_pairs={{248,0},{0,8},{8,16},{16,24},{24,32},{32,40},{40,48},{48,56},{56,6... | collective-permute-start | bytes 1572872 | tf_op jit(solution)/shard_map/ppermute | solution.py:12
  237.3 32.6 %collective-permute-start.8 = (f32[1024,128]{1,0:T(8,128)S(1)}, f32[1024,128]{1,0:T(8,128)S(1)}, u32[]{:S(2)}, u32[]{:S(2)}) collective-permute-start(f32[1024,128]{1,0:T(8,128)S(1)} %bitcast_add_fusion.5), channel_id=1, source_target_pairs={{248,0},{0,8},{8,16},{16,24},{24,32},{32,40},{40,48},{48,56},{56,6... | collective-permute-start | bytes 1572872 | tf_op jit(solution)/shard_map/ppermute | solution.py:12
  257.0 52.9 %collective-permute-start.13 = (f32[1024,128]{1,0:T(8,128)}, f32[1024,128]{1,0:T(8,128)}, u32[]{:S(2)}, u32[]{:S(2)}) collective-permute-start(f32[1024,128]{1,0:T(8,128)} %collective-permute-done.9), channel_id=1, source_target_pairs={{248,0},{0,8},{8,16},{16,24},{24,32},{32,40},{40,48},{48,56},{56,6... | collective-permute-start | bytes 1572872 | tf_op jit(solution)/shard_map/ppermute | solution.py:12
  270.0 63.9 %collective-permute-start.12 = (f32[1024,128]{1,0:T(8,128)S(1)}, f32[1024,128]{1,0:T(8,128)S(1)}, u32[]{:S(2)}, u32[]{:S(2)}) collective-permute-start(f32[1024,128]{1,0:T(8,128)S(1)} %bitcast_add_fusion.4), channel_id=1, source_target_pairs={{248,0},{0,8},{8,16},{16,24},{24,32},{32,40},{40,48},{48,56},{56,6... | collective-permute-start | bytes 1572872 | tf_op jit(solution)/shard_map/ppermute | solution.py:12
  309.9 64.5 %collective-permute-start.17 = (f32[1024,128]{1,0:T(8,128)}, f32[1024,128]{1,0:T(8,128)}, u32[]{:S(2)}, u32[]{:S(2)}) collective-permute-start(f32[1024,128]{1,0:T(8,128)} %collective-permute-done.13), channel_id=1, source_target_pairs={{248,0},{0,8},{8,16},{16,24},{24,32},{32,40},{40,48},{48,56},{56,6... | collective-permute-start | bytes 1572872 | tf_op jit(solution)/shard_map/ppermute | solution.py:12
  334.0 61.2 %collective-permute-start.16 = (f32[1024,128]{1,0:T(8,128)S(1)}, f32[1024,128]{1,0:T(8,128)S(1)}, u32[]{:S(2)}, u32[]{:S(2)}) collective-permute-start(f32[1024,128]{1,0:T(8,128)S(1)} %bitcast_add_fusion.3), channel_id=1, source_target_pairs={{248,0},{0,8},{8,16},{16,24},{24,32},{32,40},{40,48},{48,56},{56,6... | collective-permute-start | bytes 1572872 | tf_op jit(solution)/shard_map/ppermute | solution.py:12
  374.4 42.0 %collective-permute-start.21 = (f32[1024,128]{1,0:T(8,128)}, f32[1024,128]{1,0:T(8,128)}, u32[]{:S(2)}, u32[]{:S(2)}) collective-permute-start(f32[1024,128]{1,0:T(8,128)} %collective-permute-done.17), channel_id=1, source_target_pairs={{248,0},{0,8},{8,16},{16,24},{24,32},{32,40},{40,48},{48,56},{56,6... | collective-permute-start | bytes 1572872 | tf_op jit(solution)/shard_map/ppermute | solution.py:12
  395.2 47.0 %collective-permute-start.20 = (f32[1024,128]{1,0:T(8,128)S(1)}, f32[1024,128]{1,0:T(8,128)S(1)}, u32[]{:S(2)}, u32[]{:S(2)}) collective-permute-start(f32[1024,128]{1,0:T(8,128)S(1)} %bitcast_add_fusion.2), channel_id=1, source_target_pairs={{248,0},{0,8},{8,16},{16,24},{24,32},{32,40},{40,48},{48,56},{56,6... | collective-permute-start | bytes 1572872 | tf_op jit(solution)/shard_map/ppermute | solution.py:12
  416.4 37.3 %collective-permute-start.25 = (f32[1024,128]{1,0:T(8,128)}, f32[1024,128]{1,0:T(8,128)S(1)}, u32[]{:S(2)}, u32[]{:S(2)}) collective-permute-start(f32[1024,128]{1,0:T(8,128)} %collective-permute-done.21), channel_id=1, source_target_pairs={{248,0},{0,8},{8,16},{16,24},{24,32},{32,40},{40,48},{48,56},{56,6... | collective-permute-start | bytes 1572872 | tf_op jit(solution)/shard_map/ppermute | solution.py:12
  442.3 22.1 %collective-permute-start.24 = (f32[1024,128]{1,0:T(8,128)S(1)}, f32[1024,128]{1,0:T(8,128)S(1)}, u32[]{:S(2)}, u32[]{:S(2)}) collective-permute-start(f32[1024,128]{1,0:T(8,128)S(1)} %bitcast_add_fusion.1), channel_id=1, source_target_pairs={{248,0},{0,8},{8,16},{16,24},{24,32},{32,40},{40,48},{48,56},{56,6... | collective-permute-start | bytes 1572872 | tf_op jit(solution)/shard_map/ppermute | solution.py:12
  (23 other events, 254.4 us)
Sparse Core Ops, SparseCore 0:
  465.3 32.1 reduce-scatter.1
where the time goes:
time: 590 us; the launch traced here: 581 us
  waiting for transfers between devices  396 us (67%)
  blocking collectives  72.2 us (12%)
  matrix products  43.7 us (7%)
  starting transfers between devices  38 us (6%)
  between operations  15.3 us (3%)
  local copies, waits for them, and re-layouts  8.84 us (1%)
    ppermute x37, waiting for transfers between devices, passed_along(): return lax.ppermute(block, axis, route)  396 us
    ppermute x37, starting transfers between devices, passed_along(): return lax.ppermute(block, axis, route)  37.9 us
    dot_general x16, matrix products, pair_terms(): products = jnp.dot(cotangent, vectors.T, precision=lax.Precision.HIGHEST)  27.8 us
    unnamed x1, blocking collectives  22.9 us
    all_gather x1, blocking collectives, shards(): lax.all_gather(vectors, 'rows', axis=0, tiled=True)  21.3 us
    all_gather x1, blocking collectives, shards(): lax.all_gather(source_pos, 'rows', axis=1, tiled=True)  15.9 us
    dot_general x16, matrix products, pair_terms(): grad_vec = jnp.dot(kernel.T, cotangent, precision=lax.Precision.HIGHEST)  15.8 us
    all_gather x1, blocking collectives, shards(): lax.all_gather(source_len, 'rows', axis=0, tiled=True)  12 us
  transfers between devices with their start and end apart: 38, of which 29 were waited for; matrix products, arithmetic and copies ran while one was open for 9% of the time, Pallas kernels for 0%

commit v1 on v0

v1 whole, which is shorter than its diff:
```python
import functools

import jax
import jax.numpy as jnp
from jax import lax
from jax.experimental import pallas as pl
from jax.experimental.pallas import tpu as pltpu
from jax.sharding import PartitionSpec as P


F32, BF16 = jnp.float32, jnp.bfloat16
LOG2E = 1.4426950408889634
SCALE = LOG2E ** 0.5
MID = 2.51926
T_ROWS, S_ROWS, LANES = 264, 136, 128
TILE = 64


def split(x):
    hi = x.astype(BF16)
    return hi, (x - hi.astype(F32)).astype(BF16)


def split3(x):
    a = x.astype(BF16).astype(F32)
    b = (x - a).astype(BF16).astype(F32)
    return a, b, (x - a - b).astype(BF16).astype(F32)


def norm_of(x, y, z):
    return x * x + y * y + z * z


def target_rows(x, y, z):
    rows = []
    for value in (x, y, z):
        a, b, c = split3(value)
        rows += [a, b, a, c, a, b]
    rows += list(split3(norm_of(x, y, z))) + [jnp.ones_like(x)] * 3 + [jnp.zeros_like(x)] * 8
    return jnp.concatenate(rows, 0)


def source_rows(x, y, z):
    rows = []
    for value in (x, y, z):
        a, b, c = split3(value)
        rows += [2 * a, 2 * a, 2 * b, 2 * a, 2 * c, 2 * b]
    rows += [-jnp.ones_like(x)] * 3 + [-r for r in split3(norm_of(x, y, z))] + [jnp.zeros_like(x)] * 8
    return jnp.concatenate(rows, 0)


def column(row):
    return jnp.transpose(jnp.broadcast_to(row, (LANES, LANES)))


def call(body, inputs, outs, scratch=(), held=None, flops=0):
    vmem = pl.BlockSpec(memory_space=pltpu.VMEM)
    held = len(inputs) if held is None else held
    return pl.pallas_call(
        body,
        out_shape=outs,
        in_specs=[vmem] * len(inputs),
        scratch_shapes=scratch,
        cost_estimate=pl.CostEstimate(flops=flops, transcendentals=0, bytes_accessed=0),
    )(*[pltpu.with_memory_space_constraint(x, pltpu.VMEM) for x in inputs[:held]], *inputs[held:])


def pack_body(t_pos, t_len, cot, s_pos, s_len, vec, target, source):
    length = s_len[...].reshape(1, LANES)
    source[0:LANES, :] = vec[...] * column(length * jnp.sqrt(length))
    source[LANES:S_ROWS, :] = jnp.concatenate(
        [(s_pos[...] - MID) * SCALE, length * length, jnp.zeros((4, LANES), F32)], 0)
    pos = (t_pos[...] - MID) * SCALE
    meta = []
    for half in range(2):
        lanes = slice(half * LANES, (half + 1) * LANES)
        length = 2.0 * t_len[lanes].reshape(1, LANES)
        target[lanes, :] = cot[lanes, :] * column(length * jnp.sqrt(length))
        meta += [pos[:, lanes], 0.25 * length * length]
    target[2 * LANES:T_ROWS, :] = jnp.concatenate(meta, 0)


def pair_body(count, parts_n, *refs):
    parts, refs = refs[:parts_n], refs[parts_n:]
    blocks, refs = refs[:count], refs[count:]
    outs, refs = refs[:count], refs[count:]
    sums, vec3, feats, lens2, grads, rowsum, cots, prods, dists, highs, lows = refs
    blocks = [b.at[pl.ds(o, S_ROWS), :] for b in blocks for o in range(0, b.shape[0], S_ROWS)]
    outs = [b.at[pl.ds(o, S_ROWS), :] for b in outs for o in range(0, b.shape[0], S_ROWS)]
    total = len(blocks) * LANES
    width = 2 * LANES
    for k, block in enumerate(blocks):
        rows = pl.ds(k * LANES, LANES)
        hi, lo = split(block[0:LANES, :])
        vec3[rows, :] = jnp.concatenate([hi, hi, lo], 1)
        meta = block[LANES:S_ROWS, :]
        feats[rows, :] = jnp.transpose(source_rows(meta[0:1], meta[1:2], meta[2:3])).astype(BF16)
        lens2[rows, :] = column(meta[3:4])

    def first(c):
        hi, lo = split(parts[c][0:width, :])
        cots[c] = jnp.concatenate([hi, lo, hi], 1)
        meta = parts[c][width:T_ROWS, :]
        rows = [target_rows(*(meta[4 * h + r:4 * h + r + 1] for r in range(3))) for h in range(2)]
        prods[c % 2] = lax.dot_general(
            vec3[...], cots[c], (((1,), (1,)), ((), ())), preferred_element_type=F32)
        dists[c % 2] = jnp.dot(
            feats[...], jnp.concatenate(rows, 1).astype(BF16), preferred_element_type=F32)

    def middle(c):
        t_shaped = jnp.zeros((8, width), F32)
        t_weighted = jnp.zeros((8, width), F32)
        meta = parts[c][width:T_ROWS, :]
        t_len2 = jnp.concatenate([meta[3:4], meta[7:8]], 1)
        t_len2 = jnp.broadcast_to(t_len2, (TILE, width))
        for j in range(total // TILE):
            rows = pl.ds(j * TILE, TILE)
            s_len2 = lens2[rows, :]
            root = lax.rsqrt(t_len2 + jnp.concatenate([s_len2, s_len2], 1))
            inverse = root * root
            exponent = dists[c % 2, rows, :] * inverse
            kernel = (inverse * root) * jnp.exp2(exponent)
            weighted = prods[c % 2, rows, :] * kernel
            shaped = weighted * (inverse * (exponent + 1.5 * LOG2E))
            hi, lo = split(kernel)
            highs[c % 2, rows, :] = hi
            lows[c % 2, rows, :] = lo
            part = shaped[:, :LANES] + shaped[:, LANES:]
            rowsum[rows, :] = part if c == 0 else rowsum[rows, :] + part
            t_shaped += jnp.sum(shaped.reshape(TILE // 8, 8, width), 0)
            t_weighted += jnp.sum(weighted.reshape(TILE // 8, 8, width), 0)
        t_shaped = jnp.sum(t_shaped, 0, keepdims=True) * (-2.0 / LOG2E)
        t_weighted = jnp.sum(t_weighted, 0, keepdims=True)
        halves = [t_shaped[:, :LANES], t_shaped[:, LANES:], t_weighted[:, :LANES], t_weighted[:, LANES:]]
        sums[c // 2 + parts_n // 2 * (c % 2)] = jnp.concatenate(halves + [jnp.zeros((4, LANES), F32)], 0)

    def last(c):
        cot = cots[c, :, 0:width]
        part = jnp.dot(highs[c % 2], cot, preferred_element_type=F32)
        part += jnp.dot(lows[c % 2], cot, preferred_element_type=F32)
        grads[...] = part if c == 0 else grads[...] + part

    first(0)
    for c in range(parts_n):
        if c + 1 < parts_n:
            first(c + 1)
        middle(c)
        if c:
            last(c - 1)
    last(parts_n - 1)
    for k, out in enumerate(outs):
        rows = pl.ds(k * LANES, LANES)
        out[0:LANES, :] = grads[rows, :LANES] + grads[rows, LANES:]
        row = jnp.sum(jnp.transpose(rowsum[rows, :]), 0, keepdims=True) * (-2.0 / LOG2E)
        out[LANES:S_ROWS, :] = jnp.concatenate([row, jnp.zeros((7, LANES), F32)], 0)


def pair(parts, blocks):
    n = len(parts)
    total = sum(b.shape[0] for b in blocks) // S_ROWS * LANES
    width = 2 * LANES
    return call(
        functools.partial(pair_body, len(blocks), n), list(parts) + list(blocks),
        [pltpu.VMEM(b.shape, F32) for b in blocks] + [pltpu.VMEM((n, 8, LANES), F32)],
        [
            pltpu.VMEM((total, 3 * LANES), BF16), pltpu.VMEM((total, 32), BF16),
            pltpu.VMEM((total, LANES), F32), pltpu.VMEM((total, width), F32),
            pltpu.VMEM((total, LANES), F32), pltpu.VMEM((n, width, 3 * LANES), BF16),
            pltpu.VMEM((2, total, width), F32), pltpu.VMEM((2, total, width), F32),
            pltpu.VMEM((2, total, width), BF16), pltpu.VMEM((2, total, width), BF16),
        ],
        flops=8 * 10 ** 9,
    )


def finish_body(own, near1, near2, near3, far, own_sums, near_sums, s_len, vec, t_len,
                grad_vec, grad_s, grad_t):
    total = own[...] + far[...] + near1[...] + near2[...] + near3[...]
    length = s_len[...].reshape(1, LANES)
    grad = total[0:LANES, :] * column(length * jnp.sqrt(length))
    grad_vec[...] = grad
    weighted = jnp.sum(jnp.transpose(vec[...] * grad), 0, keepdims=True)
    grad_s[...] = (length * total[LANES:LANES + 1, :] + 1.5 / length * weighted).reshape(LANES)
    sums = own_sums[...] + near_sums[...]
    for half in range(2):
        lanes = slice(half * LANES, (half + 1) * LANES)
        length = t_len[lanes].reshape(1, LANES)
        grad_t[lanes] = (length * sums[half:half + 1] + 1.5 / length * sums[2 + half:3 + half]).reshape(LANES)


def send(block, axis, target):
    return lax.ppermute(block, axis, [(i, target(i)) for i in range(lax.axis_size(axis))])


def flip(block):
    return send(block, "blk", lambda i: i ^ 1)


def ahead(block, distance):
    n = lax.axis_size("blk")
    return send(block, "blk", lambda i: (i + 2 * distance) % n)


def across(block, sign):
    n = lax.axis_size("blk")
    return send(block, "blk", lambda i: i if i % 2 else (i + 8 * sign) % n)


def row_send(block, mask):
    return send(block, "rows", lambda i: i ^ mask)


def device_part(target_pos, target_len, cotangent, source_pos, source_len, vectors):
    target, source = call(
        pack_body, [target_pos, target_len, cotangent, source_pos, source_len, vectors],
        [pltpu.VMEM((T_ROWS, LANES), F32), pltpu.VMEM((S_ROWS, LANES), F32)], held=0)
    other = flip(source)
    z_parts = [target] + [row_send(target, 2 * k) for k in (1, 2, 3)]
    core_parts = [row_send(part, 1) for part in z_parts]
    parts = [part for pair_of in zip(z_parts, core_parts) for part in pair_of]
    near = [ahead(source, d) for d in (1, 2, 3)]
    far = [ahead(other, d) for d in (1, 2, 3)]

    *far_grads, g_across, sums_far = pair(parts, far + [across(other, 1)])
    far_sum = across(g_across, -1)
    for d in (3, 2, 1):
        far_sum = far_sum + ahead(far_grads[d - 1], -d)
    *near_grads, g_own, sums_near = pair(parts, near + [source])
    far_sum = flip(far_sum)
    near_grads = [ahead(near_grads[d - 1], -d) for d in (1, 2, 3)]

    sums = sums_far + sums_near
    chip = sums[0:4] + row_send(sums[4:8], 1)
    half = chip[0:2] + row_send(chip[2:4], 4)
    last = row_send(half[1], 2)

    outs = [
        jax.ShapeDtypeStruct((LANES, LANES), F32),
        jax.ShapeDtypeStruct((LANES,), F32),
        jax.ShapeDtypeStruct((2 * LANES,), F32),
    ]
    inputs = [g_own, *near_grads, far_sum, half[0], last, source_len, vectors, target_len]
    return call(finish_body, inputs, outs, held=7)


def solution(mesh):
    placed = (
        P(None, ("blk", "rows")),
        P(("blk", "rows")),
        P(("blk", "rows"), None),
        P(None, ("blk", "rows")),
        P(("blk", "rows")),
        P(("blk", "rows"), None),
    )
    return jax.shard_map(
        device_part,
        mesh=mesh,
        in_specs=placed,
        out_specs=(P(("blk", "rows"), None), P(("blk", "rows")), P(("blk", "rows"))),
        check_vma=False,
    )
```

time: 590 us -> 81.6 us (0.14)
  the two profiles are of different devices: /device:TPU:1 before, /device:TPU:62 now
where the time goes in v1:
time: 81.6 us; the launch traced here: 81.4 us
  starting transfers between devices  42.5 us (52%)
  waiting for transfers between devices  26.7 us (33%)
  Pallas kernels  11.4 us (14%)
    ppermute x26, starting transfers between devices, send(): lax.ppermute(block, axis, [(i, target(i)) for i in range(lax.axis_size(ax...  42.5 us
    ppermute x26, waiting for transfers between devices, send(): lax.ppermute(block, axis, [(i, target(i)) for i in range(lax.axis_size(ax...  26.7 us
    pallas_call x4, Pallas kernels, call(): pl.pallas_call(body, out_shape=outs, in_specs=[vmem] * len(inputs), scrat...  11.4 us
  transfers between devices with their start and end apart: 26, of which 8 were waited for; matrix products, arithmetic and copies ran while one was open for 0% of the time, Pallas kernels for 5%

profile of v1, /device:TPU:62, one launch (start us, length us, event | category | flops | bytes accessed | tf_op | source)
XLA Modules:
  0.0 81.4 jit_solution(16208998348319174049)
XLA Ops:
  0.6 1.1 %shard_map.85 = (f32[264,128]{1,0:T(8,128)S(1)}, f32[136,128]{1,0:T(8,128)S(1)}) custom-call(f32[3,256]{1,0:T(4,128)} %t_pos.1, f32[256]{0:T(256)} %t_len.3, f32[256,128]{1,0:T(8,128)} %cot.1, f32[3,128]{1,0:T(4,128)} %s_pos.1, f32[128]{0:T(128)} %s_len.3, f32[128,128]{1,0:T(8,128)} %vec.3), custom_call_target="tpu_custom_call" | custom-call | tf_op jit(solution)/shard_map/pallas_call | solution.py:59
  1.7 2.0 %collective-permute-start.5 = (f32[264,128]{1,0:T(8,128)S(1)}, f32[264,128]{1,0:T(8,128)S(1)}, u32[]{:S(2)}, u32[]{:S(2)}) collective-permute-start(f32[264,128]{1,0:T(8,128)S(1)} %get-tuple-element.15.refs_0_), channel_id=1, source_target_pairs={{0,6},{1,7},{2,4},{3,5},{4,2},{5,3},{6,0},{7,1},{8,14},{9,15},{10,... | collective-permute-start | bytes 405512 | tf_op jit(solution)/shard_map/ppermute | solution.py:192
  3.8 1.5 %collective-permute-start.3 = (f32[264,128]{1,0:T(8,128)S(1)}, f32[264,128]{1,0:T(8,128)S(1)}, u32[]{:S(2)}, u32[]{:S(2)}) collective-permute-start(f32[264,128]{1,0:T(8,128)S(1)} %get-tuple-element.15.refs_0_), channel_id=1, source_target_pairs={{0,4},{1,5},{2,6},{3,7},{4,0},{5,1},{6,2},{7,3},{8,12},{9,13},{10,... | collective-permute-start | bytes 405512 | tf_op jit(solution)/shard_map/ppermute | solution.py:192
  5.2 1.4 %collective-permute-start.1 = (f32[264,128]{1,0:T(8,128)S(1)}, f32[264,128]{1,0:T(8,128)S(1)}, u32[]{:S(2)}, u32[]{:S(2)}) collective-permute-start(f32[264,128]{1,0:T(8,128)S(1)} %get-tuple-element.15.refs_0_), channel_id=1, source_target_pairs={{0,2},{1,3},{2,0},{3,1},{4,6},{5,7},{6,4},{7,5},{8,10},{9,11},{10,... | collective-permute-start | bytes 405512 | tf_op jit(solution)/shard_map/ppermute | solution.py:192
  6.6 5.0 %collective-permute-start.13 = (f32[136,128]{1,0:T(8,128)S(1)}, f32[136,128]{1,0:T(8,128)S(1)}, u32[]{:S(2)}, u32[]{:S(2)}) collective-permute-start(f32[136,128]{1,0:T(8,128)S(1)} %get-tuple-element.16.refs_11_), channel_id=1, source_target_pairs={{0,8},{8,0},{16,24},{24,16},{32,40},{40,32},{48,56},{56,48},{64,72... | collective-permute-start | bytes 208904 | tf_op jit(solution)/shard_map/ppermute | solution.py:192
  12.1 7.0 %collective-permute-done.13 = f32[136,128]{1,0:T(8,128)S(1)} collective-permute-done((f32[136,128]{1,0:T(8,128)S(1)}, f32[136,128]{1,0:T(8,128)S(1)}, u32[]{:S(2)}, u32[]{:S(2)}) %collective-permute-start.13) | collective-permute-done | bytes 69664 | tf_op jit(solution)/shard_map/ppermute | solution.py:192
  21.2 3.7 %collective-permute-done.8.refs_9_ = f32[136,128]{1,0:T(8,128)S(1)} collective-permute-done((f32[136,128]{1,0:T(8,128)S(1)}, f32[136,128]{1,0:T(8,128)S(1)}, u32[]{:S(2)}, u32[]{:S(2)}) %collective-permute-start.8) | collective-permute-done | bytes 69664 | tf_op jit(solution)/shard_map/ppermute | solution.py:192
  24.9 2.2 %collective-permute-start.7 = (f32[136,128]{1,0:T(8,128)S(1)}, f32[136,128]{1,0:T(8,128)S(1)}, u32[]{:S(2)}, u32[]{:S(2)}) collective-permute-start(f32[136,128]{1,0:T(8,128)S(1)} %get-tuple-element.16.refs_11_), channel_id=1, source_target_pairs={{0,16},{8,24},{16,32},{24,40},{32,48},{40,56},{48,64},{56,72},{64,... | collective-permute-start | bytes 208904 | tf_op jit(solution)/shard_map/ppermute | solution.py:192
  27.1 2.1 %collective-permute-done.7.refs_8_ = f32[136,128]{1,0:T(8,128)S(1)} collective-permute-done((f32[136,128]{1,0:T(8,128)S(1)}, f32[136,128]{1,0:T(8,128)S(1)}, u32[]{:S(2)}, u32[]{:S(2)}) %collective-permute-start.7) | collective-permute-done | bytes 69664 | tf_op jit(solution)/shard_map/ppermute | solution.py:192
  29.2 2.1 %collective-permute-start.17 = (f32[136,128]{1,0:T(8,128)S(1)}, f32[136,128]{1,0:T(8,128)S(1)}, u32[]{:S(2)}, u32[]{:S(2)}) collective-permute-start(f32[136,128]{1,0:T(8,128)S(1)} %collective-permute-done.13), channel_id=1, source_target_pairs={{0,64},{8,8},{16,80},{24,24},{32,96},{40,40},{48,112},{56,56},{64,... | collective-permute-start | bytes 208904 | tf_op jit(solution)/shard_map/ppermute | solution.py:192
  31.3 1.9 %collective-permute-start.16 = (f32[136,128]{1,0:T(8,128)S(1)}, f32[136,128]{1,0:T(8,128)S(1)}, u32[]{:S(2)}, u32[]{:S(2)}) collective-permute-start(f32[136,128]{1,0:T(8,128)S(1)} %collective-permute-done.13), channel_id=1, source_target_pairs={{0,48},{8,56},{16,64},{24,72},{32,80},{40,88},{48,96},{56,104},{64... | collective-permute-start | bytes 208904 | tf_op jit(solution)/shard_map/ppermute | solution.py:192
  33.2 5.1 %collective-permute-start.15 = (f32[136,128]{1,0:T(8,128)S(1)}, f32[136,128]{1,0:T(8,128)S(1)}, u32[]{:S(2)}, u32[]{:S(2)}) collective-permute-start(f32[136,128]{1,0:T(8,128)S(1)} %collective-permute-done.13), channel_id=1, source_target_pairs={{0,32},{8,40},{16,48},{24,56},{32,64},{40,72},{48,80},{56,88},{64,... | collective-permute-start | bytes 208904 | tf_op jit(solution)/shard_map/ppermute | solution.py:192
  38.4 4.3 %shard_map.86 = (f32[136,128]{1,0:T(8,128)S(1)}, f32[136,128]{1,0:T(8,128)S(1)}, f32[136,128]{1,0:T(8,128)S(1)}, f32[136,128]{1,0:T(8,128)S(1)}, f32[8,8,128]{2,1,0:T(8,128)S(1)}) custom-call(f32[264,128]{1,0:T(8,128)S(1)} %get-tuple-element.15.refs_0_, f32[264,128]{1,0:T(8,128)S(1)} %collective-permute-done.refs_1_, ...), custom_call_target="tpu_custom_call" | custom-call | flops 8000000000 | tf_op jit(solution)/shard_map/pallas_call | solution.py:59
  42.8 4.3 %shard_map.87 = (f32[136,128]{1,0:T(8,128)S(1)}, f32[136,128]{1,0:T(8,128)S(1)}, f32[136,128]{1,0:T(8,128)S(1)}, f32[136,128]{1,0:T(8,128)S(1)}, f32[8,8,128]{2,1,0:T(8,128)S(1)}) custom-call(f32[264,128]{1,0:T(8,128)S(1)} %get-tuple-element.15.refs_0_, f32[264,128]{1,0:T(8,128)S(1)} %collective-permute-done.refs_1_, ...), custom_call_target="tpu_custom_call" | custom-call | flops 8000000000 | tf_op jit(solution)/shard_map/pallas_call | solution.py:59
  47.2 1.2 %collective-permute-done.23 = f32[4,8,128]{2,1,0:T(8,128)S(1)} collective-permute-done((f32[4,8,128]{2,1,0:T(8,128)S(1)}, f32[4,8,128]{2,1,0:T(8,128)S(1)}, u32[]{:S(2)}, u32[]{:S(2)}) %collective-permute-start.23) | collective-permute-done | bytes 16416 | tf_op jit(solution)/shard_map/ppermute | solution.py:192
  48.4 4.7 %collective-permute-start.24 = (f32[2,8,128]{2,1,0:T(8,128)S(1)}, f32[2,8,128]{2,1,0:T(8,128)S(1)}, u32[]{:S(2)}, u32[]{:S(2)}) collective-permute-start(f32[2,8,128]{2,1,0:T(8,128)S(1)} %slice.27), channel_id=1, source_target_pairs={{0,4},{1,5},{2,6},{3,7},{4,0},{5,1},{6,2},{7,3},{8,12},{9,13},{10,... | collective-permute-start | bytes 24584 | tf_op jit(solution)/shard_map/ppermute | solution.py:192
  53.1 3.2 %collective-permute-start.18 = (f32[136,128]{1,0:T(8,128)S(1)}, f32[136,128]{1,0:T(8,128)S(1)}, u32[]{:S(2)}, u32[]{:S(2)}) collective-permute-start(f32[136,128]{1,0:T(8,128)S(1)} %get-tuple-element.21), channel_id=1, source_target_pairs={{0,192},{8,8},{16,208},{24,24},{32,224},{40,40},{48,240},{56,56},{... | collective-permute-start | bytes 208904 | tf_op jit(solution)/shard_map/ppermute | solution.py:192
  56.3 2.6 %collective-permute-start.19 = (f32[136,128]{1,0:T(8,128)S(1)}, f32[136,128]{1,0:T(8,128)S(1)}, u32[]{:S(2)}, u32[]{:S(2)}) collective-permute-start(f32[136,128]{1,0:T(8,128)S(1)} %get-tuple-element.22), channel_id=1, source_target_pairs={{0,208},{8,216},{16,224},{24,232},{32,240},{40,248},{48,0},{56,8},... | collective-permute-start | bytes 208904 | tf_op jit(solution)/shard_map/ppermute | solution.py:192
  59.0 3.0 %collective-permute-start.20 = (f32[136,128]{1,0:T(8,128)S(1)}, f32[136,128]{1,0:T(8,128)S(1)}, u32[]{:S(2)}, u32[]{:S(2)}) collective-permute-start(f32[136,128]{1,0:T(8,128)S(1)} %get-tuple-element.23), channel_id=1, source_target_pairs={{0,224},{8,232},{16,240},{24,248},{32,0},{40,8},{48,16},{56,24},{6... | collective-permute-start | bytes 208904 | tf_op jit(solution)/shard_map/ppermute | solution.py:192
  61.9 4.1 %collective-permute-start.11 = (f32[136,128]{1,0:T(8,128)S(1)}, f32[136,128]{1,0:T(8,128)S(1)}, u32[]{:S(2)}, u32[]{:S(2)}) collective-permute-start(f32[136,128]{1,0:T(8,128)S(1)} %get-tuple-element.19), channel_id=1, source_target_pairs={{0,224},{8,232},{16,240},{24,248},{32,0},{40,8},{48,16},{56,24},{6... | collective-permute-start | bytes 208904 | tf_op jit(solution)/shard_map/ppermute | solution.py:192
  67.2 3.8 %collective-permute-done.21 = f32[136,128]{1,0:T(8,128)S(1)} collective-permute-done((f32[136,128]{1,0:T(8,128)S(1)}, f32[136,128]{1,0:T(8,128)S(1)}, u32[]{:S(2)}, u32[]{:S(2)}) %collective-permute-start.21) | collective-permute-done | bytes 69664 | tf_op jit(solution)/shard_map/ppermute | solution.py:192
  71.3 3.6 %collective-permute-done.25.near_sums = f32[8,128]{1,0:T(8,128)S(1)} collective-permute-done((f32[8,128]{1,0:T(8,128)S(1)}, f32[8,128]{1,0:T(8,128)S(1)}, u32[]{:S(2)}, u32[]{:S(2)}) %collective-permute-start.25) | collective-permute-done | bytes 4128 | tf_op jit(solution)/shard_map/ppermute | solution.py:192
  74.9 4.9 %collective-permute-done.22.far = f32[136,128]{1,0:T(8,128)S(1)} collective-permute-done((f32[136,128]{1,0:T(8,128)S(1)}, f32[136,128]{1,0:T(8,128)S(1)}, u32[]{:S(2)}, u32[]{:S(2)}) %collective-permute-start.22) | collective-permute-done | bytes 69664 | tf_op jit(solution)/shard_map/ppermute | solution.py:192
  79.8 1.6 %shard_map.88 = (f32[128,128]{1,0:T(8,128)}, f32[128]{0:T(128)}, f32[256]{0:T(256)}) custom-call(f32[136,128]{1,0:T(8,128)S(1)} %get-tuple-element.17.own, f32[136,128]{1,0:T(8,128)S(1)} %collective-permute-done.10.near1, f32[136,128]{1,0:T(8,128)S(1)} %collective-permute-done.11.near2, f32[136,128]{1,0:T(8,128)S(1)} %collective-permute-done.12.near3, ...), custom_call_target="tpu_custom_call" | custom-call | tf_op jit(solution)/shard_map/pallas_call | solution.py:59
  (39 shorter events, 4.1 us)
Async XLA Ops:
  1.7 18.4 %collective-permute-start.5 = (f32[264,128]{1,0:T(8,128)S(1)}, f32[264,128]{1,0:T(8,128)S(1)}, u32[]{:S(2)}, u32[]{:S(2)}) collective-permute-start(f32[264,128]{1,0:T(8,128)S(1)} %get-tuple-element.15.refs_0_), channel_id=1, source_target_pairs={{0,6},{1,7},{2,4},{3,5},{4,2},{5,3},{6,0},{7,1},{8,14},{9,15},{10,... | collective-permute-start | bytes 405512 | tf_op jit(solution)/shard_map/ppermute | solution.py:192
  3.8 16.9 %collective-permute-start.3 = (f32[264,128]{1,0:T(8,128)S(1)}, f32[264,128]{1,0:T(8,128)S(1)}, u32[]{:S(2)}, u32[]{:S(2)}) collective-permute-start(f32[264,128]{1,0:T(8,128)S(1)} %get-tuple-element.15.refs_0_), channel_id=1, source_target_pairs={{0,4},{1,5},{2,6},{3,7},{4,0},{5,1},{6,2},{7,3},{8,12},{9,13},{10,... | collective-permute-start | bytes 405512 | tf_op jit(solution)/shard_map/ppermute | solution.py:192
  5.2 15.5 %collective-permute-start.1 = (f32[264,128]{1,0:T(8,128)S(1)}, f32[264,128]{1,0:T(8,128)S(1)}, u32[]{:S(2)}, u32[]{:S(2)}) collective-permute-start(f32[264,128]{1,0:T(8,128)S(1)} %get-tuple-element.15.refs_0_), channel_id=1, source_target_pairs={{0,2},{1,3},{2,0},{3,1},{4,6},{5,7},{6,4},{7,5},{8,10},{9,11},{10,... | collective-permute-start | bytes 405512 | tf_op jit(solution)/shard_map/ppermute | solution.py:192
  6.6 12.5 %collective-permute-start.13 = (f32[136,128]{1,0:T(8,128)S(1)}, f32[136,128]{1,0:T(8,128)S(1)}, u32[]{:S(2)}, u32[]{:S(2)}) collective-permute-start(f32[136,128]{1,0:T(8,128)S(1)} %get-tuple-element.16.refs_11_), channel_id=1, source_target_pairs={{0,8},{8,0},{16,24},{24,16},{32,40},{40,32},{48,56},{56,48},{64,72... | collective-permute-start | bytes 208904 | tf_op jit(solution)/shard_map/ppermute | solution.py:192
  11.6 8.5 %collective-permute-start.9 = (f32[136,128]{1,0:T(8,128)S(1)}, f32[136,128]{1,0:T(8,128)S(1)}, u32[]{:S(2)}, u32[]{:S(2)}) collective-permute-start(f32[136,128]{1,0:T(8,128)S(1)} %get-tuple-element.16.refs_11_), channel_id=1, source_target_pairs={{0,48},{8,56},{16,64},{24,72},{32,80},{40,88},{48,96},{56,104},{64... | collective-permute-start | bytes 208904 | tf_op jit(solution)/shard_map/ppermute | solution.py:192
  19.1 5.8 %collective-permute-start.8 = (f32[136,128]{1,0:T(8,128)S(1)}, f32[136,128]{1,0:T(8,128)S(1)}, u32[]{:S(2)}, u32[]{:S(2)}) collective-permute-start(f32[136,128]{1,0:T(8,128)S(1)} %get-tuple-element.16.refs_11_), channel_id=1, source_target_pairs={{0,32},{8,40},{16,48},{24,56},{32,64},{40,72},{48,80},{56,88},{64,... | collective-permute-start | bytes 208904 | tf_op jit(solution)/shard_map/ppermute | solution.py:192
  20.1 11.2 %collective-permute-start = (f32[264,128]{1,0:T(8,128)S(1)}, f32[264,128]{1,0:T(8,128)S(1)}, u32[]{:S(2)}, u32[]{:S(2)}) collective-permute-start(f32[264,128]{1,0:T(8,128)S(1)} %get-tuple-element.15.refs_0_), channel_id=1, source_target_pairs={{0,1},{1,0},{2,3},{3,2},{4,5},{5,4},{6,7},{7,6},{8,9},{9,8},{10,11... | collective-permute-start | bytes 405512 | tf_op jit(solution)/shard_map/ppermute | solution.py:192
  20.1 13.1 %collective-permute-start.6 = (f32[264,128]{1,0:T(8,128)S(1)}, f32[264,128]{1,0:T(8,128)S(1)}, u32[]{:S(2)}, u32[]{:S(2)}) collective-permute-start(f32[264,128]{1,0:T(8,128)S(1)} %collective-permute-done.5.refs_6_), channel_id=1, source_target_pairs={{0,1},{1,0},{2,3},{3,2},{4,5},{5,4},{6,7},{7,6},{8,9},{9,8},{10,11... | collective-permute-start | bytes 405512 | tf_op jit(solution)/shard_map/ppermute | solution.py:192
  20.6 17.7 %collective-permute-start.4 = (f32[264,128]{1,0:T(8,128)S(1)}, f32[264,128]{1,0:T(8,128)S(1)}, u32[]{:S(2)}, u32[]{:S(2)}) collective-permute-start(f32[264,128]{1,0:T(8,128)S(1)} %collective-permute-done.3.refs_4_), channel_id=1, source_target_pairs={{0,1},{1,0},{2,3},{3,2},{4,5},{5,4},{6,7},{7,6},{8,9},{9,8},{10,11... | collective-permute-start | bytes 405512 | tf_op jit(solution)/shard_map/ppermute | solution.py:192
  20.7 17.6 %collective-permute-start.2 = (f32[264,128]{1,0:T(8,128)S(1)}, f32[264,128]{1,0:T(8,128)S(1)}, u32[]{:S(2)}, u32[]{:S(2)}) collective-permute-start(f32[264,128]{1,0:T(8,128)S(1)} %collective-permute-done.1.refs_2_), channel_id=1, source_target_pairs={{0,1},{1,0},{2,3},{3,2},{4,5},{5,4},{6,7},{7,6},{8,9},{9,8},{10,11... | collective-permute-start | bytes 405512 | tf_op jit(solution)/shard_map/ppermute | solution.py:192
  24.9 4.3 %collective-permute-start.7 = (f32[136,128]{1,0:T(8,128)S(1)}, f32[136,128]{1,0:T(8,128)S(1)}, u32[]{:S(2)}, u32[]{:S(2)}) collective-permute-start(f32[136,128]{1,0:T(8,128)S(1)} %get-tuple-element.16.refs_11_), channel_id=1, source_target_pairs={{0,16},{8,24},{16,32},{24,40},{32,48},{40,56},{48,64},{56,72},{64,... | collective-permute-start | bytes 208904 | tf_op jit(solution)/shard_map/ppermute | solution.py:192
  29.2 13.6 %collective-permute-start.17 = (f32[136,128]{1,0:T(8,128)S(1)}, f32[136,128]{1,0:T(8,128)S(1)}, u32[]{:S(2)}, u32[]{:S(2)}) collective-permute-start(f32[136,128]{1,0:T(8,128)S(1)} %collective-permute-done.13), channel_id=1, source_target_pairs={{0,64},{8,8},{16,80},{24,24},{32,96},{40,40},{48,112},{56,56},{64,... | collective-permute-start | bytes 208904 | tf_op jit(solution)/shard_map/ppermute | solution.py:192
  31.3 11.4 %collective-permute-start.16 = (f32[136,128]{1,0:T(8,128)S(1)}, f32[136,128]{1,0:T(8,128)S(1)}, u32[]{:S(2)}, u32[]{:S(2)}) collective-permute-start(f32[136,128]{1,0:T(8,128)S(1)} %collective-permute-done.13), channel_id=1, source_target_pairs={{0,48},{8,56},{16,64},{24,72},{32,80},{40,88},{48,96},{56,104},{64... | collective-permute-start | bytes 208904 | tf_op jit(solution)/shard_map/ppermute | solution.py:192
  33.2 9.5 %collective-permute-start.15 = (f32[136,128]{1,0:T(8,128)S(1)}, f32[136,128]{1,0:T(8,128)S(1)}, u32[]{:S(2)}, u32[]{:S(2)}) collective-permute-start(f32[136,128]{1,0:T(8,128)S(1)} %collective-permute-done.13), channel_id=1, source_target_pairs={{0,32},{8,40},{16,48},{24,56},{32,64},{40,72},{48,80},{56,88},{64,... | collective-permute-start | bytes 208904 | tf_op jit(solution)/shard_map/ppermute | solution.py:192
  38.4 4.4 %collective-permute-start.14 = (f32[136,128]{1,0:T(8,128)S(1)}, f32[136,128]{1,0:T(8,128)S(1)}, u32[]{:S(2)}, u32[]{:S(2)}) collective-permute-start(f32[136,128]{1,0:T(8,128)S(1)} %collective-permute-done.13), channel_id=1, source_target_pairs={{0,16},{8,24},{16,32},{24,40},{32,48},{40,56},{48,64},{56,72},{64,... | collective-permute-start | bytes 208904 | tf_op jit(solution)/shard_map/ppermute | solution.py:192
  48.4 13.5 %collective-permute-start.24 = (f32[2,8,128]{2,1,0:T(8,128)S(1)}, f32[2,8,128]{2,1,0:T(8,128)S(1)}, u32[]{:S(2)}, u32[]{:S(2)}) collective-permute-start(f32[2,8,128]{2,1,0:T(8,128)S(1)} %slice.27), channel_id=1, source_target_pairs={{0,4},{1,5},{2,6},{3,7},{4,0},{5,1},{6,2},{7,3},{8,12},{9,13},{10,... | collective-permute-start | bytes 24584 | tf_op jit(solution)/shard_map/ppermute | solution.py:192
  53.1 8.9 %collective-permute-start.18 = (f32[136,128]{1,0:T(8,128)S(1)}, f32[136,128]{1,0:T(8,128)S(1)}, u32[]{:S(2)}, u32[]{:S(2)}) collective-permute-start(f32[136,128]{1,0:T(8,128)S(1)} %get-tuple-element.21), channel_id=1, source_target_pairs={{0,192},{8,8},{16,208},{24,24},{32,224},{40,40},{48,240},{56,56},{... | collective-permute-start | bytes 208904 | tf_op jit(solution)/shard_map/ppermute | solution.py:192
  56.3 9.8 %collective-permute-start.19 = (f32[136,128]{1,0:T(8,128)S(1)}, f32[136,128]{1,0:T(8,128)S(1)}, u32[]{:S(2)}, u32[]{:S(2)}) collective-permute-start(f32[136,128]{1,0:T(8,128)S(1)} %get-tuple-element.22), channel_id=1, source_target_pairs={{0,208},{8,216},{16,224},{24,232},{32,240},{40,248},{48,0},{56,8},... | collective-permute-start | bytes 208904 | tf_op jit(solution)/shard_map/ppermute | solution.py:192
  59.0 8.3 %collective-permute-start.20 = (f32[136,128]{1,0:T(8,128)S(1)}, f32[136,128]{1,0:T(8,128)S(1)}, u32[]{:S(2)}, u32[]{:S(2)}) collective-permute-start(f32[136,128]{1,0:T(8,128)S(1)} %get-tuple-element.23), channel_id=1, source_target_pairs={{0,224},{8,232},{16,240},{24,248},{32,0},{40,8},{48,16},{56,24},{6... | collective-permute-start | bytes 208904 | tf_op jit(solution)/shard_map/ppermute | solution.py:192
  61.9 9.1 %collective-permute-start.21 = (f32[136,128]{1,0:T(8,128)S(1)}, f32[136,128]{1,0:T(8,128)S(1)}, u32[]{:S(2)}, u32[]{:S(2)}) collective-permute-start(f32[136,128]{1,0:T(8,128)S(1)} %get-tuple-element.24), channel_id=1, source_target_pairs={{0,240},{8,248},{16,0},{24,8},{32,16},{40,24},{48,32},{56,40},{64,... | collective-permute-start | bytes 208904 | tf_op jit(solution)/shard_map/ppermute | solution.py:192
  61.9 13.0 %collective-permute-start.10 = (f32[136,128]{1,0:T(8,128)S(1)}, f32[136,128]{1,0:T(8,128)S(1)}, u32[]{:S(2)}, u32[]{:S(2)}) collective-permute-start(f32[136,128]{1,0:T(8,128)S(1)} %get-tuple-element.18), channel_id=1, source_target_pairs={{0,240},{8,248},{16,0},{24,8},{32,16},{40,24},{48,32},{56,40},{64,... | collective-permute-start | bytes 208904 | tf_op jit(solution)/shard_map/ppermute | solution.py:192
  61.9 12.9 %collective-permute-start.11 = (f32[136,128]{1,0:T(8,128)S(1)}, f32[136,128]{1,0:T(8,128)S(1)}, u32[]{:S(2)}, u32[]{:S(2)}) collective-permute-start(f32[136,128]{1,0:T(8,128)S(1)} %get-tuple-element.19), channel_id=1, source_target_pairs={{0,224},{8,232},{16,240},{24,248},{32,0},{40,8},{48,16},{56,24},{6... | collective-permute-start | bytes 208904 | tf_op jit(solution)/shard_map/ppermute | solution.py:192
  66.1 8.8 %collective-permute-start.12 = (f32[136,128]{1,0:T(8,128)S(1)}, f32[136,128]{1,0:T(8,128)S(1)}, u32[]{:S(2)}, u32[]{:S(2)}) collective-permute-start(f32[136,128]{1,0:T(8,128)S(1)} %get-tuple-element.20), channel_id=1, source_target_pairs={{0,208},{8,216},{16,224},{24,232},{32,240},{40,248},{48,0},{56,8},... | collective-permute-start | bytes 208904 | tf_op jit(solution)/shard_map/ppermute | solution.py:192
  71.1 8.8 %collective-permute-start.22 = (f32[136,128]{1,0:T(8,128)S(1)}, f32[136,128]{1,0:T(8,128)S(1)}, u32[]{:S(2)}, u32[]{:S(2)}) collective-permute-start(f32[136,128]{1,0:T(8,128)S(1)} %add_add_fusion), channel_id=1, source_target_pairs={{0,8},{8,0},{16,24},{24,16},{32,40},{40,32},{48,56},{56,48},{64,72... | collective-permute-start | bytes 208904 | tf_op jit(solution)/shard_map/ppermute | solution.py:192
  (2 other events, 5.0 us)

commit v2 on v1

--- a/solution.py
+++ b/solution.py
@@ -65,8 +65,10 @@
     )(*[pltpu.with_memory_space_constraint(x, pltpu.VMEM) for x in inputs[:held]], *inputs[held:])
 
 
-def pack_body(t_pos, t_len, cot, s_pos, s_len, vec, target, source):
+def pack_body(t_pos, t_len, cot, s_pos, s_len, vec, target, source, kept, lens):
     length = s_len[...].reshape(1, LANES)
+    kept[...] = vec[...]
+    lens[0:1, :] = length
     source[0:LANES, :] = vec[...] * column(length * jnp.sqrt(length))
     source[LANES:S_ROWS, :] = jnp.concatenate(
         [(s_pos[...] - MID) * SCALE, length * length, jnp.zeros((4, LANES), F32)], 0)
@@ -74,20 +76,22 @@
     meta = []
     for half in range(2):
         lanes = slice(half * LANES, (half + 1) * LANES)
-        length = 2.0 * t_len[lanes].reshape(1, LANES)
+        lens[1 + half:2 + half, :] = t_len[lanes].reshape(1, LANES)
+        length = 2.0 * lens[1 + half:2 + half, :]
         target[lanes, :] = cot[lanes, :] * column(length * jnp.sqrt(length))
         meta += [pos[:, lanes], 0.25 * length * length]
     target[2 * LANES:T_ROWS, :] = jnp.concatenate(meta, 0)
 
 
-def pair_body(count, parts_n, *refs):
+def pair_body(count, parts_n, before, *refs):
     parts, refs = refs[:parts_n], refs[parts_n:]
     blocks, refs = refs[:count], refs[count:]
+    if before:
+        earlier, refs = refs[:count], refs[count:]
+        far_sums, early_sums, refs = refs[0], refs[1], refs[2:]
     outs, refs = refs[:count], refs[count:]
     sums, vec3, feats, lens2, grads, rowsum, cots, prods, dists, highs, lows = refs
-    blocks = [b.at[pl.ds(o, S_ROWS), :] for b in blocks for o in range(0, b.shape[0], S_ROWS)]
-    outs = [b.at[pl.ds(o, S_ROWS), :] for b in outs for o in range(0, b.shape[0], S_ROWS)]
-    total = len(blocks) * LANES
+    total = count * LANES
     width = 2 * LANES
     for k, block in enumerate(blocks):
         rows = pl.ds(k * LANES, LANES)
@@ -132,7 +136,13 @@
         t_shaped = jnp.sum(t_shaped, 0, keepdims=True) * (-2.0 / LOG2E)
         t_weighted = jnp.sum(t_weighted, 0, keepdims=True)
         halves = [t_shaped[:, :LANES], t_shaped[:, LANES:], t_weighted[:, :LANES], t_weighted[:, LANES:]]
-        sums[c // 2 + parts_n // 2 * (c % 2)] = jnp.concatenate(halves + [jnp.zeros((4, LANES), F32)], 0)
+        row = jnp.concatenate(halves + [jnp.zeros((4, LANES), F32)], 0)
+        if before:
+            row += far_sums[parts_n + c]
+            sums[c % 2, (parts_n + c) // 2] = row
+            sums[c % 2, c // 2] = far_sums[c] + early_sums[c]
+        else:
+            sums[c] = row
 
     def last(c):
         cot = cots[c, :, 0:width]
@@ -150,18 +160,24 @@
     last(parts_n - 1)
     for k, out in enumerate(outs):
         rows = pl.ds(k * LANES, LANES)
-        out[0:LANES, :] = grads[rows, :LANES] + grads[rows, LANES:]
+        grad = grads[rows, :LANES] + grads[rows, LANES:]
         row = jnp.sum(jnp.transpose(rowsum[rows, :]), 0, keepdims=True) * (-2.0 / LOG2E)
-        out[LANES:S_ROWS, :] = jnp.concatenate([row, jnp.zeros((7, LANES), F32)], 0)
-
-
-def pair(parts, blocks):
-    n = len(parts)
-    total = sum(b.shape[0] for b in blocks) // S_ROWS * LANES
+        row = jnp.concatenate([row, jnp.zeros((7, LANES), F32)], 0)
+        if before:
+            grad += earlier[k][0:LANES, :]
+            row += earlier[k][LANES:S_ROWS, :]
+        out[0:LANES, :] = grad
+        out[LANES:S_ROWS, :] = row
+
+
+def pair(parts, blocks, before=()):
+    n, count = len(parts), len(blocks)
+    total = count * LANES
     width = 2 * LANES
+    sums = (2, n, 8, LANES) if before else (n, 8, LANES)
     return call(
-        functools.partial(pair_body, len(blocks), n), list(parts) + list(blocks),
-        [pltpu.VMEM(b.shape, F32) for b in blocks] + [pltpu.VMEM((n, 8, LANES), F32)],
+        functools.partial(pair_body, count, n, bool(before)), [*parts, *blocks, *before],
+        [pltpu.VMEM((S_ROWS, LANES), F32)] * count + [pltpu.VMEM(sums, F32)],
         [
             pltpu.VMEM((total, 3 * LANES), BF16), pltpu.VMEM((total, 32), BF16),
             pltpu.VMEM((total, LANES), F32), pltpu.VMEM((total, width), F32),
@@ -169,14 +185,14 @@
             pltpu.VMEM((2, total, width), F32), pltpu.VMEM((2, total, width), F32),
             pltpu.VMEM((2, total, width), BF16), pltpu.VMEM((2, total, width), BF16),
         ],
-        flops=8 * 10 ** 9,
+        flops=2 * n * count * 10 ** 8,
     )
 
 
-def finish_body(own, near1, near2, near3, far, own_sums, near_sums, s_len, vec, t_len,
+def finish_body(own, near1, near2, near3, far, own_sums, near_sums, vec, lens,
                 grad_vec, grad_s, grad_t):
     total = own[...] + far[...] + near1[...] + near2[...] + near3[...]
-    length = s_len[...].reshape(1, LANES)
+    length = lens[0:1, :]
     grad = total[0:LANES, :] * column(length * jnp.sqrt(length))
     grad_vec[...] = grad
     weighted = jnp.sum(jnp.transpose(vec[...] * grad), 0, keepdims=True)
@@ -184,7 +200,7 @@
     sums = own_sums[...] + near_sums[...]
     for half in range(2):
         lanes = slice(half * LANES, (half + 1) * LANES)
-        length = t_len[lanes].reshape(1, LANES)
+        length = lens[1 + half:2 + half, :]
         grad_t[lanes] = (length * sums[half:half + 1] + 1.5 / length * sums[2 + half:3 + half]).reshape(LANES)
 
 
@@ -211,26 +227,25 @@
 
 
 def device_part(target_pos, target_len, cotangent, source_pos, source_len, vectors):
-    target, source = call(
+    target, source, kept, lens = call(
         pack_body, [target_pos, target_len, cotangent, source_pos, source_len, vectors],
-        [pltpu.VMEM((T_ROWS, LANES), F32), pltpu.VMEM((S_ROWS, LANES), F32)], held=0)
+        [pltpu.VMEM((rows, LANES), F32) for rows in (T_ROWS, S_ROWS, LANES, 8)], held=0)
     other = flip(source)
     z_parts = [target] + [row_send(target, 2 * k) for k in (1, 2, 3)]
     core_parts = [row_send(part, 1) for part in z_parts]
     parts = [part for pair_of in zip(z_parts, core_parts) for part in pair_of]
-    near = [ahead(source, d) for d in (1, 2, 3)]
-    far = [ahead(other, d) for d in (1, 2, 3)]
-
-    *far_grads, g_across, sums_far = pair(parts, far + [across(other, 1)])
-    far_sum = across(g_across, -1)
-    for d in (3, 2, 1):
-        far_sum = far_sum + ahead(far_grads[d - 1], -d)
-    *near_grads, g_own, sums_near = pair(parts, near + [source])
-    far_sum = flip(far_sum)
+    near = [ahead(source, d) for d in (1, 2, 3)] + [source]
+    far = [ahead(other, d) for d in (1, 2, 3)] + [across(other, 1)]
+
+    *early_grads, early_sums = pair(parts[:4], near)
+    *far_grads, far_sums = pair(parts, far)
+    far_grads = [ahead(far_grads[d - 1], -d) for d in (1, 2, 3)] + [
+        across(far_grads[3], -1)]
+    *near_grads, g_own, sums = pair(parts[4:], near, [*early_grads, far_sums, early_sums])
+    far_grad = flip(far_grads[0] + far_grads[1] + far_grads[2] + far_grads[3])
     near_grads = [ahead(near_grads[d - 1], -d) for d in (1, 2, 3)]
 
-    sums = sums_far + sums_near
-    chip = sums[0:4] + row_send(sums[4:8], 1)
+    chip = sums[0] + row_send(sums[1], 1)
     half = chip[0:2] + row_send(chip[2:4], 4)
     last = row_send(half[1], 2)
 
@@ -239,8 +254,7 @@
         jax.ShapeDtypeStruct((LANES,), F32),
         jax.ShapeDtypeStruct((2 * LANES,), F32),
     ]
-    inputs = [g_own, *near_grads, far_sum, half[0], last, source_len, vectors, target_len]
-    return call(finish_body, inputs, outs, held=7)
+    return call(finish_body, [g_own, *near_grads, far_grad, half[0], last, kept, lens], outs)
 
 
 def solution(mesh):

time: 81.6 us -> 70.6 us (0.87)
  the two profiles are of different devices: /device:TPU:62 before, /device:TPU:40 now
where the time goes in v2:
time: 70.6 us; the launch traced here: 70.5 us
  starting transfers between devices  43.2 us (61%)
  waiting for transfers between devices  15.5 us (22%)
  Pallas kernels  11 us (16%)
  between operations  0.75 us (1%)
    ppermute x26, starting transfers between devices, send(): lax.ppermute(block, axis, [(i, target(i)) for i in range(lax.axis_size(ax...  43.2 us
    ppermute x26, waiting for transfers between devices, send(): lax.ppermute(block, axis, [(i, target(i)) for i in range(lax.axis_size(ax...  15.5 us
    pallas_call x5, Pallas kernels, call(): pl.pallas_call(body, out_shape=outs, in_specs=[vmem] * len(inputs), scrat...  11 us
  transfers between devices with their start and end apart: 26, of which 8 were waited for; matrix products, arithmetic and copies ran while one was open for 0% of the time, Pallas kernels for 3%

profile of v2, /device:TPU:40, one launch (start us, length us, event | category | flops | bytes accessed | tf_op | source)
XLA Modules:
  0.0 70.5 jit_solution(13671668989922823649)
XLA Ops:
  0.6 1.1 %shard_map.85 = (f32[264,128]{1,0:T(8,128)S(1)}, f32[136,128]{1,0:T(8,128)S(1)}, f32[128,128]{1,0:T(8,128)S(1)}, f32[8,128]{1,0:T(8,128)S(1)}) custom-call(f32[3,256]{1,0:T(4,128)} %t_pos.1, f32[256]{0:T(256)} %t_len.1, f32[256,128]{1,0:T(8,128)} %cot.1, f32[3,128]{1,0:T(4,128)} %s_pos.1, f32[128]{0:T(128)} %s_len.1, f32[128,128]{1,0:T(8,128)} %vec.1), custom_call_target="tpu_custom_call" | custom-call | tf_op jit(solution)/shard_map/pallas_call | solution.py:59
  1.9 7.2 %collective-permute-start.10 = (f32[136,128]{1,0:T(8,128)S(1)}, f32[136,128]{1,0:T(8,128)S(1)}, u32[]{:S(2)}, u32[]{:S(2)}) collective-permute-start(f32[136,128]{1,0:T(8,128)S(1)} %get-tuple-element.23.refs_7_), channel_id=1, source_target_pairs={{0,8},{8,0},{16,24},{24,16},{32,40},{40,32},{48,56},{56,48},{64,72... | collective-permute-start | bytes 208904 | tf_op jit(solution)/shard_map/ppermute | solution.py:208
  9.1 2.8 %collective-permute-start.6 = (f32[136,128]{1,0:T(8,128)S(1)}, f32[136,128]{1,0:T(8,128)S(1)}, u32[]{:S(2)}, u32[]{:S(2)}) collective-permute-start(f32[136,128]{1,0:T(8,128)S(1)} %get-tuple-element.23.refs_7_), channel_id=1, source_target_pairs={{0,48},{8,56},{16,64},{24,72},{32,80},{40,88},{48,96},{56,104},{64... | collective-permute-start | bytes 208904 | tf_op jit(solution)/shard_map/ppermute | solution.py:208
  11.9 1.8 %collective-permute-start.5 = (f32[136,128]{1,0:T(8,128)S(1)}, f32[136,128]{1,0:T(8,128)S(1)}, u32[]{:S(2)}, u32[]{:S(2)}) collective-permute-start(f32[136,128]{1,0:T(8,128)S(1)} %get-tuple-element.23.refs_7_), channel_id=1, source_target_pairs={{0,32},{8,40},{16,48},{24,56},{32,64},{40,72},{48,80},{56,88},{64,... | collective-permute-start | bytes 208904 | tf_op jit(solution)/shard_map/ppermute | solution.py:208
  15.3 1.0 %collective-permute-start.2 = (f32[264,128]{1,0:T(8,128)S(1)}, f32[264,128]{1,0:T(8,128)S(1)}, u32[]{:S(2)}, u32[]{:S(2)}) collective-permute-start(f32[264,128]{1,0:T(8,128)S(1)} %get-tuple-element.22.refs_0_), channel_id=1, source_target_pairs={{0,6},{1,7},{2,4},{3,5},{4,2},{5,3},{6,0},{7,1},{8,14},{9,15},{10,... | collective-permute-start | bytes 405512 | tf_op jit(solution)/shard_map/ppermute | solution.py:208
  16.4 2.3 %collective-permute-done.5.refs_5_ = f32[136,128]{1,0:T(8,128)S(1)} collective-permute-done((f32[136,128]{1,0:T(8,128)S(1)}, f32[136,128]{1,0:T(8,128)S(1)}, u32[]{:S(2)}, u32[]{:S(2)}) %collective-permute-start.5) | collective-permute-done | bytes 69664 | tf_op jit(solution)/shard_map/ppermute | solution.py:208
  18.6 1.5 %collective-permute-start = (f32[264,128]{1,0:T(8,128)S(1)}, f32[264,128]{1,0:T(8,128)S(1)}, u32[]{:S(2)}, u32[]{:S(2)}) collective-permute-start(f32[264,128]{1,0:T(8,128)S(1)} %get-tuple-element.22.refs_0_), channel_id=1, source_target_pairs={{0,4},{1,5},{2,6},{3,7},{4,0},{5,1},{6,2},{7,3},{8,12},{9,13},{10,... | collective-permute-start | bytes 405512 | tf_op jit(solution)/shard_map/ppermute | solution.py:208
  20.1 3.5 %collective-permute-start.14 = (f32[136,128]{1,0:T(8,128)S(1)}, f32[136,128]{1,0:T(8,128)S(1)}, u32[]{:S(2)}, u32[]{:S(2)}) collective-permute-start(f32[136,128]{1,0:T(8,128)S(1)} %collective-permute-done.10), channel_id=1, source_target_pairs={{0,64},{8,8},{16,80},{24,24},{32,96},{40,40},{48,112},{56,56},{64,... | collective-permute-start | bytes 208904 | tf_op jit(solution)/shard_map/ppermute | solution.py:208
  23.6 1.5 %collective-permute-start.13 = (f32[136,128]{1,0:T(8,128)S(1)}, f32[136,128]{1,0:T(8,128)S(1)}, u32[]{:S(2)}, u32[]{:S(2)}) collective-permute-start(f32[136,128]{1,0:T(8,128)S(1)} %collective-permute-done.10), channel_id=1, source_target_pairs={{0,48},{8,56},{16,64},{24,72},{32,80},{40,88},{48,96},{56,104},{64... | collective-permute-start | bytes 208904 | tf_op jit(solution)/shard_map/ppermute | solution.py:208
  25.1 2.5 %collective-permute-done.2.refs_6_.refs_2_ = f32[264,128]{1,0:T(8,128)S(1)} collective-permute-done((f32[264,128]{1,0:T(8,128)S(1)}, f32[264,128]{1,0:T(8,128)S(1)}, u32[]{:S(2)}, u32[]{:S(2)}) %collective-permute-start.2) | collective-permute-done | bytes 135200 | tf_op jit(solution)/shard_map/ppermute | solution.py:208
  27.6 3.0 %collective-permute-start.12 = (f32[136,128]{1,0:T(8,128)S(1)}, f32[136,128]{1,0:T(8,128)S(1)}, u32[]{:S(2)}, u32[]{:S(2)}) collective-permute-start(f32[136,128]{1,0:T(8,128)S(1)} %collective-permute-done.10), channel_id=1, source_target_pairs={{0,32},{8,40},{16,48},{24,56},{32,64},{40,72},{48,80},{56,88},{64,... | collective-permute-start | bytes 208904 | tf_op jit(solution)/shard_map/ppermute | solution.py:208
  31.8 2.4 %shard_map.86 = (f32[136,128]{1,0:T(8,128)S(1)}, f32[136,128]{1,0:T(8,128)S(1)}, f32[136,128]{1,0:T(8,128)S(1)}, f32[136,128]{1,0:T(8,128)S(1)}, f32[4,8,128]{2,1,0:T(8,128)S(1)}) custom-call(f32[264,128]{1,0:T(8,128)S(1)} %get-tuple-element.22.refs_0_, f32[264,128]{1,0:T(8,128)S(1)} %collective-permute-done.7.refs_1_, ...), custom_call_target="tpu_custom_call" | custom-call | flops 3200000000 | tf_op jit(solution)/shard_map/pallas_call | solution.py:59
  35.0 2.0 %collective-permute-done.11.refs_8_ = f32[136,128]{1,0:T(8,128)S(1)} collective-permute-done((f32[136,128]{1,0:T(8,128)S(1)}, f32[136,128]{1,0:T(8,128)S(1)}, u32[]{:S(2)}, u32[]{:S(2)}) %collective-permute-start.11) | collective-permute-done | bytes 69664 | tf_op jit(solution)/shard_map/ppermute | solution.py:208
  37.0 4.3 %shard_map.87 = (f32[136,128]{1,0:T(8,128)S(1)}, f32[136,128]{1,0:T(8,128)S(1)}, f32[136,128]{1,0:T(8,128)S(1)}, f32[136,128]{1,0:T(8,128)S(1)}, f32[8,8,128]{2,1,0:T(8,128)S(1)}) custom-call(f32[264,128]{1,0:T(8,128)S(1)} %get-tuple-element.22.refs_0_, f32[264,128]{1,0:T(8,128)S(1)} %collective-permute-done.7.refs_1_, ...), custom_call_target="tpu_custom_call" | custom-call | flops 6400000000 | tf_op jit(solution)/shard_map/pallas_call | solution.py:59
  41.4 2.4 %shard_map.88 = (f32[136,128]{1,0:T(8,128)S(1)}, f32[136,128]{1,0:T(8,128)S(1)}, f32[136,128]{1,0:T(8,128)S(1)}, f32[136,128]{1,0:T(8,128)S(1)}, f32[2,4,8,128]{3,2,1,0:T(8,128)S(1)}) custom-call(f32[264,128]{1,0:T(8,128)S(1)} %collective-permute-done.refs_4_.refs_0_, f32[264,128]{1,0:T(8,128)S(1)} %collective-permute-done.1.refs_5_.refs_1_, ...), custom_call_target="tpu_custom_call" | custom-call | flops 3200000000 | tf_op jit(solution)/shard_map/pallas_call | solution.py:59
  43.9 1.2 %collective-permute-done.23 = f32[4,8,128]{2,1,0:T(8,128)S(1)} collective-permute-done((f32[4,8,128]{2,1,0:T(8,128)S(1)}, f32[4,8,128]{2,1,0:T(8,128)S(1)}, u32[]{:S(2)}, u32[]{:S(2)}) %collective-permute-start.23) | collective-permute-done | bytes 16416 | tf_op jit(solution)/shard_map/ppermute | solution.py:208
  45.1 1.4 %collective-permute-start.24 = (f32[2,8,128]{2,1,0:T(8,128)S(1)}, f32[2,8,128]{2,1,0:T(8,128)S(1)}, u32[]{:S(2)}, u32[]{:S(2)}) collective-permute-start(f32[2,8,128]{2,1,0:T(8,128)S(1)} %slice.25), channel_id=1, source_target_pairs={{0,4},{1,5},{2,6},{3,7},{4,0},{5,1},{6,2},{7,3},{8,12},{9,13},{10,... | collective-permute-start | bytes 24584 | tf_op jit(solution)/shard_map/ppermute | solution.py:208
  47.8 3.8 %collective-permute-start.19 = (f32[136,128]{1,0:T(8,128)S(1)}, f32[136,128]{1,0:T(8,128)S(1)}, u32[]{:S(2)}, u32[]{:S(2)}) collective-permute-start(f32[136,128]{1,0:T(8,128)S(1)} %get-tuple-element.35), channel_id=1, source_target_pairs={{0,224},{8,232},{16,240},{24,248},{32,0},{40,8},{48,16},{56,24},{6... | collective-permute-start | bytes 208904 | tf_op jit(solution)/shard_map/ppermute | solution.py:208
  51.8 3.5 %collective-permute-start.21 = (f32[136,128]{1,0:T(8,128)S(1)}, f32[136,128]{1,0:T(8,128)S(1)}, u32[]{:S(2)}, u32[]{:S(2)}) collective-permute-start(f32[136,128]{1,0:T(8,128)S(1)} %get-tuple-element.37), channel_id=1, source_target_pairs={{0,192},{8,8},{16,208},{24,24},{32,224},{40,40},{48,240},{56,56},{... | collective-permute-start | bytes 208904 | tf_op jit(solution)/shard_map/ppermute | solution.py:208
  55.4 3.0 %collective-permute-start.16 = (f32[136,128]{1,0:T(8,128)S(1)}, f32[136,128]{1,0:T(8,128)S(1)}, u32[]{:S(2)}, u32[]{:S(2)}) collective-permute-start(f32[136,128]{1,0:T(8,128)S(1)} %get-tuple-element.32), channel_id=1, source_target_pairs={{0,224},{8,232},{16,240},{24,248},{32,0},{40,8},{48,16},{56,24},{6... | collective-permute-start | bytes 208904 | tf_op jit(solution)/shard_map/ppermute | solution.py:208
  58.4 2.9 %collective-permute-start.17 = (f32[136,128]{1,0:T(8,128)S(1)}, f32[136,128]{1,0:T(8,128)S(1)}, u32[]{:S(2)}, u32[]{:S(2)}) collective-permute-start(f32[136,128]{1,0:T(8,128)S(1)} %get-tuple-element.33), channel_id=1, source_target_pairs={{0,208},{8,216},{16,224},{24,232},{32,240},{40,248},{48,0},{56,8},... | collective-permute-start | bytes 208904 | tf_op jit(solution)/shard_map/ppermute | solution.py:208
  61.3 2.4 %collective-permute-start.22 = (f32[136,128]{1,0:T(8,128)S(1)}, f32[136,128]{1,0:T(8,128)S(1)}, u32[]{:S(2)}, u32[]{:S(2)}) collective-permute-start(f32[136,128]{1,0:T(8,128)S(1)} %add_add_fusion), channel_id=1, source_target_pairs={{0,8},{8,0},{16,24},{24,16},{32,40},{40,32},{48,56},{56,48},{64,72... | collective-permute-start | bytes 208904 | tf_op jit(solution)/shard_map/ppermute | solution.py:208
  63.7 3.6 %collective-permute-done.25.near_sums = f32[8,128]{1,0:T(8,128)S(1)} collective-permute-done((f32[8,128]{1,0:T(8,128)S(1)}, f32[8,128]{1,0:T(8,128)S(1)}, u32[]{:S(2)}, u32[]{:S(2)}) %collective-permute-start.25) | collective-permute-done | bytes 4128 | tf_op jit(solution)/shard_map/ppermute | solution.py:208
  67.3 2.4 %collective-permute-done.22.far = f32[136,128]{1,0:T(8,128)S(1)} collective-permute-done((f32[136,128]{1,0:T(8,128)S(1)}, f32[136,128]{1,0:T(8,128)S(1)}, u32[]{:S(2)}, u32[]{:S(2)}) %collective-permute-start.22) | collective-permute-done | bytes 69664 | tf_op jit(solution)/shard_map/ppermute | solution.py:208
  (39 shorter events, 6.3 us)
Async XLA Ops:
  1.8 18.3 %collective-permute-start.8 = (f32[264,128]{1,0:T(8,128)S(1)}, f32[264,128]{1,0:T(8,128)S(1)}, u32[]{:S(2)}, u32[]{:S(2)}) collective-permute-start(f32[264,128]{1,0:T(8,128)S(1)} %get-tuple-element.22.refs_0_), channel_id=1, source_target_pairs={{0,2},{1,3},{2,0},{3,1},{4,6},{5,7},{6,4},{7,5},{8,10},{9,11},{10,... | collective-permute-start | bytes 405512 | tf_op jit(solution)/shard_map/ppermute | solution.py:208
  1.9 13.4 %collective-permute-start.10 = (f32[136,128]{1,0:T(8,128)S(1)}, f32[136,128]{1,0:T(8,128)S(1)}, u32[]{:S(2)}, u32[]{:S(2)}) collective-permute-start(f32[136,128]{1,0:T(8,128)S(1)} %get-tuple-element.23.refs_7_), channel_id=1, source_target_pairs={{0,8},{8,0},{16,24},{24,16},{32,40},{40,32},{48,56},{56,48},{64,72... | collective-permute-start | bytes 208904 | tf_op jit(solution)/shard_map/ppermute | solution.py:208
  9.1 6.2 %collective-permute-start.6 = (f32[136,128]{1,0:T(8,128)S(1)}, f32[136,128]{1,0:T(8,128)S(1)}, u32[]{:S(2)}, u32[]{:S(2)}) collective-permute-start(f32[136,128]{1,0:T(8,128)S(1)} %get-tuple-element.23.refs_7_), channel_id=1, source_target_pairs={{0,48},{8,56},{16,64},{24,72},{32,80},{40,88},{48,96},{56,104},{64... | collective-permute-start | bytes 208904 | tf_op jit(solution)/shard_map/ppermute | solution.py:208
  11.9 6.7 %collective-permute-start.5 = (f32[136,128]{1,0:T(8,128)S(1)}, f32[136,128]{1,0:T(8,128)S(1)}, u32[]{:S(2)}, u32[]{:S(2)}) collective-permute-start(f32[136,128]{1,0:T(8,128)S(1)} %get-tuple-element.23.refs_7_), channel_id=1, source_target_pairs={{0,32},{8,40},{16,48},{24,56},{32,64},{40,72},{48,80},{56,88},{64,... | collective-permute-start | bytes 208904 | tf_op jit(solution)/shard_map/ppermute | solution.py:208
  13.7 6.4 %collective-permute-start.4 = (f32[136,128]{1,0:T(8,128)S(1)}, f32[136,128]{1,0:T(8,128)S(1)}, u32[]{:S(2)}, u32[]{:S(2)}) collective-permute-start(f32[136,128]{1,0:T(8,128)S(1)} %get-tuple-element.23.refs_7_), channel_id=1, source_target_pairs={{0,16},{8,24},{16,32},{24,40},{32,48},{40,56},{48,64},{56,72},{64,... | collective-permute-start | bytes 208904 | tf_op jit(solution)/shard_map/ppermute | solution.py:208
  15.3 8.3 %collective-permute-start.7 = (f32[264,128]{1,0:T(8,128)S(1)}, f32[264,128]{1,0:T(8,128)S(1)}, u32[]{:S(2)}, u32[]{:S(2)}) collective-permute-start(f32[264,128]{1,0:T(8,128)S(1)} %get-tuple-element.22.refs_0_), channel_id=1, source_target_pairs={{0,1},{1,0},{2,3},{3,2},{4,5},{5,4},{6,7},{7,6},{8,9},{9,8},{10,11... | collective-permute-start | bytes 405512 | tf_op jit(solution)/shard_map/ppermute | solution.py:208
  15.3 12.3 %collective-permute-start.2 = (f32[264,128]{1,0:T(8,128)S(1)}, f32[264,128]{1,0:T(8,128)S(1)}, u32[]{:S(2)}, u32[]{:S(2)}) collective-permute-start(f32[264,128]{1,0:T(8,128)S(1)} %get-tuple-element.22.refs_0_), channel_id=1, source_target_pairs={{0,6},{1,7},{2,4},{3,5},{4,2},{5,3},{6,0},{7,1},{8,14},{9,15},{10,... | collective-permute-start | bytes 405512 | tf_op jit(solution)/shard_map/ppermute | solution.py:208
  18.6 12.0 %collective-permute-start = (f32[264,128]{1,0:T(8,128)S(1)}, f32[264,128]{1,0:T(8,128)S(1)}, u32[]{:S(2)}, u32[]{:S(2)}) collective-permute-start(f32[264,128]{1,0:T(8,128)S(1)} %get-tuple-element.22.refs_0_), channel_id=1, source_target_pairs={{0,4},{1,5},{2,6},{3,7},{4,0},{5,1},{6,2},{7,3},{8,12},{9,13},{10,... | collective-permute-start | bytes 405512 | tf_op jit(solution)/shard_map/ppermute | solution.py:208
  20.1 11.2 %collective-permute-start.9 = (f32[264,128]{1,0:T(8,128)S(1)}, f32[264,128]{1,0:T(8,128)S(1)}, u32[]{:S(2)}, u32[]{:S(2)}) collective-permute-start(f32[264,128]{1,0:T(8,128)S(1)} %collective-permute-done.8.refs_2_), channel_id=1, source_target_pairs={{0,1},{1,0},{2,3},{3,2},{4,5},{5,4},{6,7},{7,6},{8,9},{9,8},{10,11... | collective-permute-start | bytes 405512 | tf_op jit(solution)/shard_map/ppermute | solution.py:208
  20.1 11.2 %collective-permute-start.14 = (f32[136,128]{1,0:T(8,128)S(1)}, f32[136,128]{1,0:T(8,128)S(1)}, u32[]{:S(2)}, u32[]{:S(2)}) collective-permute-start(f32[136,128]{1,0:T(8,128)S(1)} %collective-permute-done.10), channel_id=1, source_target_pairs={{0,64},{8,8},{16,80},{24,24},{32,96},{40,40},{48,112},{56,56},{64,... | collective-permute-start | bytes 208904 | tf_op jit(solution)/shard_map/ppermute | solution.py:208
  23.6 10.6 %collective-permute-start.13 = (f32[136,128]{1,0:T(8,128)S(1)}, f32[136,128]{1,0:T(8,128)S(1)}, u32[]{:S(2)}, u32[]{:S(2)}) collective-permute-start(f32[136,128]{1,0:T(8,128)S(1)} %collective-permute-done.10), channel_id=1, source_target_pairs={{0,48},{8,56},{16,64},{24,72},{32,80},{40,88},{48,96},{56,104},{64... | collective-permute-start | bytes 208904 | tf_op jit(solution)/shard_map/ppermute | solution.py:208
  27.6 7.4 %collective-permute-start.12 = (f32[136,128]{1,0:T(8,128)S(1)}, f32[136,128]{1,0:T(8,128)S(1)}, u32[]{:S(2)}, u32[]{:S(2)}) collective-permute-start(f32[136,128]{1,0:T(8,128)S(1)} %collective-permute-done.10), channel_id=1, source_target_pairs={{0,32},{8,40},{16,48},{24,56},{32,64},{40,72},{48,80},{56,88},{64,... | collective-permute-start | bytes 208904 | tf_op jit(solution)/shard_map/ppermute | solution.py:208
  30.6 6.4 %collective-permute-start.11 = (f32[136,128]{1,0:T(8,128)S(1)}, f32[136,128]{1,0:T(8,128)S(1)}, u32[]{:S(2)}, u32[]{:S(2)}) collective-permute-start(f32[136,128]{1,0:T(8,128)S(1)} %collective-permute-done.10), channel_id=1, source_target_pairs={{0,16},{8,24},{16,32},{24,40},{32,48},{40,56},{48,64},{56,72},{64,... | collective-permute-start | bytes 208904 | tf_op jit(solution)/shard_map/ppermute | solution.py:208
  31.3 5.7 %collective-permute-start.3 = (f32[264,128]{1,0:T(8,128)S(1)}, f32[264,128]{1,0:T(8,128)S(1)}, u32[]{:S(2)}, u32[]{:S(2)}) collective-permute-start(f32[264,128]{1,0:T(8,128)S(1)} %collective-permute-done.2.refs_6_.refs_2_), channel_id=1, source_target_pairs={{0,1},{1,0},{2,3},{3,2},{4,5},{5,4},{6,7},{7,6},{8,9},{9,8},{10,11... | collective-permute-start | bytes 405512 | tf_op jit(solution)/shard_map/ppermute | solution.py:208
  31.3 5.7 %collective-permute-start.1 = (f32[264,128]{1,0:T(8,128)S(1)}, f32[264,128]{1,0:T(8,128)S(1)}, u32[]{:S(2)}, u32[]{:S(2)}) collective-permute-start(f32[264,128]{1,0:T(8,128)S(1)} %collective-permute-done.refs_4_.refs_0_), channel_id=1, source_target_pairs={{0,1},{1,0},{2,3},{3,2},{4,5},{5,4},{6,7},{7,6},{8,9},{9,8},{10,11... | collective-permute-start | bytes 405512 | tf_op jit(solution)/shard_map/ppermute | solution.py:208
  45.1 6.7 %collective-permute-start.24 = (f32[2,8,128]{2,1,0:T(8,128)S(1)}, f32[2,8,128]{2,1,0:T(8,128)S(1)}, u32[]{:S(2)}, u32[]{:S(2)}) collective-permute-start(f32[2,8,128]{2,1,0:T(8,128)S(1)} %slice.25), channel_id=1, source_target_pairs={{0,4},{1,5},{2,6},{3,7},{4,0},{5,1},{6,2},{7,3},{8,12},{9,13},{10,... | collective-permute-start | bytes 24584 | tf_op jit(solution)/shard_map/ppermute | solution.py:208
  46.4 20.9 %collective-permute-start.15 = (f32[136,128]{1,0:T(8,128)S(1)}, f32[136,128]{1,0:T(8,128)S(1)}, u32[]{:S(2)}, u32[]{:S(2)}) collective-permute-start(f32[136,128]{1,0:T(8,128)S(1)} %get-tuple-element.31), channel_id=1, source_target_pairs={{0,240},{8,248},{16,0},{24,8},{32,16},{40,24},{48,32},{56,40},{64,... | collective-permute-start | bytes 208904 | tf_op jit(solution)/shard_map/ppermute | solution.py:208
  47.1 8.2 %collective-permute-start.18 = (f32[136,128]{1,0:T(8,128)S(1)}, f32[136,128]{1,0:T(8,128)S(1)}, u32[]{:S(2)}, u32[]{:S(2)}) collective-permute-start(f32[136,128]{1,0:T(8,128)S(1)} %get-tuple-element.34), channel_id=1, source_target_pairs={{0,240},{8,248},{16,0},{24,8},{32,16},{40,24},{48,32},{56,40},{64,... | collective-permute-start | bytes 208904 | tf_op jit(solution)/shard_map/ppermute | solution.py:208
  47.8 10.6 %collective-permute-start.19 = (f32[136,128]{1,0:T(8,128)S(1)}, f32[136,128]{1,0:T(8,128)S(1)}, u32[]{:S(2)}, u32[]{:S(2)}) collective-permute-start(f32[136,128]{1,0:T(8,128)S(1)} %get-tuple-element.35), channel_id=1, source_target_pairs={{0,224},{8,232},{16,240},{24,248},{32,0},{40,8},{48,16},{56,24},{6... | collective-permute-start | bytes 208904 | tf_op jit(solution)/shard_map/ppermute | solution.py:208
  51.6 9.7 %collective-permute-start.20 = (f32[136,128]{1,0:T(8,128)S(1)}, f32[136,128]{1,0:T(8,128)S(1)}, u32[]{:S(2)}, u32[]{:S(2)}) collective-permute-start(f32[136,128]{1,0:T(8,128)S(1)} %get-tuple-element.36), channel_id=1, source_target_pairs={{0,208},{8,216},{16,224},{24,232},{32,240},{40,248},{48,0},{56,8},... | collective-permute-start | bytes 208904 | tf_op jit(solution)/shard_map/ppermute | solution.py:208
  51.8 9.5 %collective-permute-start.21 = (f32[136,128]{1,0:T(8,128)S(1)}, f32[136,128]{1,0:T(8,128)S(1)}, u32[]{:S(2)}, u32[]{:S(2)}) collective-permute-start(f32[136,128]{1,0:T(8,128)S(1)} %get-tuple-element.37), channel_id=1, source_target_pairs={{0,192},{8,8},{16,208},{24,24},{32,224},{40,40},{48,240},{56,56},{... | collective-permute-start | bytes 208904 | tf_op jit(solution)/shard_map/ppermute | solution.py:208
  55.4 12.0 %collective-permute-start.16 = (f32[136,128]{1,0:T(8,128)S(1)}, f32[136,128]{1,0:T(8,128)S(1)}, u32[]{:S(2)}, u32[]{:S(2)}) collective-permute-start(f32[136,128]{1,0:T(8,128)S(1)} %get-tuple-element.32), channel_id=1, source_target_pairs={{0,224},{8,232},{16,240},{24,248},{32,0},{40,8},{48,16},{56,24},{6... | collective-permute-start | bytes 208904 | tf_op jit(solution)/shard_map/ppermute | solution.py:208
  58.4 9.0 %collective-permute-start.17 = (f32[136,128]{1,0:T(8,128)S(1)}, f32[136,128]{1,0:T(8,128)S(1)}, u32[]{:S(2)}, u32[]{:S(2)}) collective-permute-start(f32[136,128]{1,0:T(8,128)S(1)} %get-tuple-element.33), channel_id=1, source_target_pairs={{0,208},{8,216},{16,224},{24,232},{32,240},{40,248},{48,0},{56,8},... | collective-permute-start | bytes 208904 | tf_op jit(solution)/shard_map/ppermute | solution.py:208
  61.3 8.4 %collective-permute-start.22 = (f32[136,128]{1,0:T(8,128)S(1)}, f32[136,128]{1,0:T(8,128)S(1)}, u32[]{:S(2)}, u32[]{:S(2)}) collective-permute-start(f32[136,128]{1,0:T(8,128)S(1)} %add_add_fusion), channel_id=1, source_target_pairs={{0,8},{8,0},{16,24},{24,16},{32,40},{40,32},{48,56},{56,48},{64,72... | collective-permute-start | bytes 208904 | tf_op jit(solution)/shard_map/ppermute | solution.py:208
  (2 other events, 4.9 us)
